TPU v7x, 512 devices: a whole 4x4x16 slice. The times are simulated.
512 devices in a mesh: coil: 16 (over x, z_hi, core), slab: 32 (over y, z_lo).
Axes of the slice: x: 4, y: 4, z: 16 (z_hi: 2, z_lo: 8; z = z_hi * 8 + z_lo), core: 2. Of those that a mesh axis runs over, the one named last changes fastest.
Arguments:
- kspace: bfloat16 [2, 32, 2, 32, 384, 128], P(None, 'coil', None, None, 'slab'), may hold values from -6 to 6
- coil_maps: bfloat16 [2, 32, 32, 384, 384], P(None, 'coil', None, 'slab'), may hold values from -1.1953125 to 1.1953125
- line_index: int32 [2, 384, 128], P(None, 'slab'), may hold values from 0 to 383, as said below
Outputs:
- harmonic_image: float32 [32, 2, 384, 384], P('coil', None, 'slab')
Inputs may be any that keep to these rules, and one draw needn't show every extreme that they name: `line_index`: for each phase offset and kz plane the 128 ky indices are distinct.
All inputs are finite; a program needn't handle non-finite values.
Results may differ from a plain program's by a relative error of at most 0.0043.
Values may be sent and summed in bfloat16 or wider, within the bound.
No kernel may reach another device: no remote copies, remote signals or barrier semaphores. Data moves between devices by JAX's collectives and lax.ppermute only.
A program may use at most 64 MiB of HBM per device.

v0:
```python
import math

import jax
import jax.numpy as jnp
from jax import lax
from jax.sharding import PartitionSpec as P

NY = 384
NZ = 384
PHASES = 8


def in_blocks(shard, dim, devices):
    before, after = (shard.shape[:dim], shard.shape[dim + 1 :])
    return jnp.moveaxis(shard.reshape(*before, devices, -1, *after), dim, 0)


def summed_on_arrival(shard, axis, dim):
    blocks = in_blocks(shard, dim, lax.axis_size(axis))
    arrived = lax.all_to_all(blocks, axis, split_axis=0, concat_axis=0, tiled=True)
    return arrived.sum(axis=0)


def line_tables(line_index, length):
    positions = lax.broadcasted_iota(jnp.int32, (1, 1, 1, length), 3)
    turn_count = line_index[..., None] * positions % length
    angles = turn_count.astype(jnp.float32) * (2.0 * math.pi / length)
    scaling = 1.0 / math.sqrt(length)
    return (
        (jnp.cos(angles) * scaling).astype(jnp.bfloat16),
        (jnp.sin(angles) * scaling).astype(jnp.bfloat16),
    )


def dense_tables(length):
    row_pos = lax.broadcasted_iota(jnp.int32, (length, length), 0)
    col_pos = lax.broadcasted_iota(jnp.int32, (length, length), 1)
    turn_count = row_pos * col_pos % length
    angles = turn_count.astype(jnp.float32) * (2.0 * math.pi / length)
    scaling = 1.0 / math.sqrt(length)
    return (
        (jnp.cos(angles) * scaling).astype(jnp.bfloat16),
        (jnp.sin(angles) * scaling).astype(jnp.bfloat16),
    )


def fold_offsets(real_part, imag_part, fold_axis):
    sum_real = None
    sum_imag = None
    for offset in range(real_part.shape[fold_axis]):
        phase_angle = 2.0 * math.pi * offset / PHASES
        cosine = math.cos(phase_angle)
        sine = math.sin(phase_angle)
        here_real = jnp.take(real_part, offset, axis=fold_axis)
        here_imag = jnp.take(imag_part, offset, axis=fold_axis)
        term_real = cosine * here_real + sine * here_imag
        term_imag = cosine * here_imag - sine * here_real
        if sum_real is None:
            sum_real, sum_imag = (term_real, term_imag)
        else:
            sum_real, sum_imag = (sum_real + term_real, sum_imag + term_imag)
    return jnp.stack([sum_real, sum_imag]).astype(jnp.bfloat16)


def lines_to_rows(left, right):
    return jnp.einsum("ctxkl,tkly->ctxky", left, right, preferred_element_type=jnp.float32)


def depth_pass(harmonic, depth_cos, depth_sin):

    def along(left, right):
        return jnp.einsum("cxky,kz->cxyz", left, right, preferred_element_type=jnp.float32)

    image_real = along(harmonic[0], depth_cos) - along(harmonic[1], depth_sin)
    image_imag = along(harmonic[0], depth_sin) + along(harmonic[1], depth_cos)
    return jnp.stack([image_real, image_imag])


def combine_coils(image, maps):
    add_real = jnp.sum(maps[0] * image[0] + maps[1] * image[1], axis=0)
    add_imag = jnp.sum(maps[0] * image[1] - maps[1] * image[0], axis=0)
    return jnp.stack([add_real, add_imag], axis=1)


def local(kspace, coil_maps, line_index):
    line_cos, line_sin = line_tables(line_index, NY)
    sample_real = kspace[0]
    sample_imag = kspace[1]
    hybrid_real = lines_to_rows(sample_real, line_cos) - lines_to_rows(sample_imag, line_sin)
    hybrid_imag = lines_to_rows(sample_real, line_sin) + lines_to_rows(sample_imag, line_cos)
    depth_cos, depth_sin = dense_tables(NZ)
    folded = fold_offsets(hybrid_real, hybrid_imag, 1)
    gathered = lax.all_to_all(folded, "slab", split_axis=4, concat_axis=3, tiled=True)
    maps = coil_maps.astype(jnp.float32)
    return summed_on_arrival(
        combine_coils(depth_pass(gathered, depth_cos, depth_sin), maps), "coil", 0
    )


def solution(mesh):
    placed = (
        P(None, "coil", None, None, "slab", None),
        P(None, "coil", None, "slab", None),
        P(None, "slab", None),
    )
    return jax.shard_map(
        local, mesh=mesh, in_specs=placed, out_specs=P("coil", None, "slab", None), check_vma=False
    )
```

profile of v0, /device:TPU:33, one launch (start us, length us, event | category | flops | bytes accessed | tf_op | source)
XLA Modules:
  0.0 308.2 jit_solution(15905848800679179640)
XLA Ops:
  0.0 0.7 copy.19
  0.7 1.2 fusion.69
  1.9 23.5 %fusion.9 = f32[2,12,384,2,32]{2,4,3,1,0:T(8,128)S(1)} fusion(s32[2,12,128]{2,1,0:T(8,128)S(1)} %copy.19, bf16[1,2,2,32,12,128]{5,3,4,2,1,0:T(8,128)(2,1)S(1)} %get-tuple-element.36), kind=kOutput, calls=%fused_computation.14 | convolution fusion | flops 163971072 | bytes 2764800 | tf_op jit(solution)/shard_map/ctxkl,tkly->ctxky/dot_general | solution.py:66
  25.4 23.5 %fusion.7 = f32[2,12,384,2,32]{2,4,3,1,0:T(8,128)S(1)} fusion(s32[2,12,128]{2,1,0:T(8,128)S(1)} %copy.19, bf16[1,2,2,32,12,128]{5,3,4,2,1,0:T(8,128)(2,1)S(1)} %get-tuple-element.35), kind=kOutput, calls=%fused_computation.13 | convolution fusion | flops 163971072 | bytes 2764800 | tf_op jit(solution)/shard_map/ctxkl,tkly->ctxky/dot_general | solution.py:66
  48.9 23.5 %subtract_bitcast_fusion = f32[2,2,32,12,384]{4,2,0,3,1:T(8,128)S(1)} fusion(f32[2,12,384,2,32]{2,4,3,1,0:T(8,128)S(1)} %fusion.9, s32[2,12,128]{2,1,0:T(8,128)S(1)} %copy.19, bf16[1,2,2,32,12,128]{5,3,4,2,1,0:T(8,128)(2,1)S(1)} %get-tuple-element.35), kind=kOutput, calls=%fused_computation.12 | convolution fusion | flops 164560896 | bytes 5124096 | tf_op jit(solution)/shard_map/ctxkl,tkly->ctxky/dot_general | solution.py:66
  72.3 23.5 %add_bitcast_fusion = f32[2,2,32,12,384]{4,2,0,3,1:T(8,128)S(1)} fusion(f32[2,12,384,2,32]{2,4,3,1,0:T(8,128)S(1)} %fusion.7, s32[2,12,128]{2,1,0:T(8,128)S(1)} %copy.19, bf16[1,2,2,32,12,128]{5,3,4,2,1,0:T(8,128)(2,1)S(1)} %get-tuple-element.36), kind=kOutput, calls=%fused_computation.11 | convolution fusion | flops 164560896 | bytes 5124096 | tf_op jit(solution)/shard_map/ctxkl,tkly->ctxky/dot_general | solution.py:66
  95.8 0.6 fusion.25
  96.4 0.1 pad_maximum_fusion
  96.6 8.6 %copy.22 = bf16[2,2,32,12,384]{2,1,3,0,4:T(2,128)(2,1)} copy(bf16[2,2,32,12,384]{4,2,1,3,0:T(8,128)(2,1)S(1)} %pad_maximum_fusion) | data formatting | bytes 2359296 | tf_op jit(solution)/shard_map/stack | solution.py:62
  105.1 10.8 %reshape.84 = bf16[32,2,9216]{2,1,0:T(2,128)(2,1)} reshape(bf16[384,2,12,2,32]{4,3,2,1,0:T(2,128)(2,1)} %bitcast.118) | data formatting | bytes 2359296
  116.0 0.0 copy-start.2
  116.0 15.0 %all-to-all-start = ((bf16[32,2,9216]{2,1,0:T(2,128)(2,1)}), bf16[32,2,9216]{2,1,0:T(2,128)(2,1)S(1)}, u32[]{:S(2)}, u32[]{:S(2)}) async-start(bf16[32,2,9216]{2,1,0:T(2,128)(2,1)} %reshape.84), calls=%async_computation | async-start | bytes 2359296 | tf_op jit(solution)/shard_map/all_to_all | solution.py:93
  131.0 0.0 copy-done.2
  131.0 1.7 convert_element_type.32
  132.7 54.7 %all-to-all-done = bf16[32,2,9216]{2,1,0:T(2,128)(2,1)S(1)} async-done(((bf16[32,2,9216]{2,1,0:T(2,128)(2,1)}), bf16[32,2,9216]{2,1,0:T(2,128)(2,1)S(1)}, u32[]{:S(2)}, u32[]{:S(2)}) %all-to-all-start) | async-done | bytes 1179680 | tf_op jit(solution)/shard_map/all_to_all | solution.py:93
  187.4 3.9 %reshape.85 = bf16[384,2,12,2,32]{4,3,2,1,0:T(2,128)(2,1)} reshape(bf16[32,2,9216]{2,1,0:T(2,128)(2,1)S(1)} %all-to-all-done) | data formatting | bytes 2359296
  191.3 9.3 %copy.23 = bf16[2,2,32,12,384]{2,1,4,3,0:T(2,128)(2,1)} copy(bf16[2,2,32,12,384]{2,1,3,0,4:T(2,128)(2,1)} %bitcast.119) | data formatting | bytes 2359296 | tf_op jit(solution)/shard_map/all_to_all | solution.py:93
  200.6 7.1 %fusion.68 = (bf16[1,2,32,32,12,12]{2,1,5,3,4,0:T(2,128)(2,1)}, bf16[1,2,32,32,12,12]{2,1,5,3,4,0:T(2,128)(2,1)S(1)}) fusion(bf16[2,2,32,32,12,12]{2,1,5,3,4,0:T(2,128)(2,1)} %bitcast.117), kind=kLoop, calls=%fused_computation.82 | loop fusion | bytes 2359296 | tf_op jit(solution)/shard_map/slice | solution.py:74
  207.6 1.6 copy.24
  209.2 2.2 copy.25
  211.4 0.0 copy-start
  211.4 3.6 %fusion.34 = f32[2,32,12,384]{3,1,2,0:T(8,128)} fusion(bf16[2,32,384,12]{2,1,3,0:T(8,128)(2,1)S(1)} %copy.25), kind=kOutput, calls=%fused_computation.49 | convolution fusion | flops 228114432 | bytes 1769472 | tf_op jit(solution)/shard_map/cxky,kz->cxyz/dot_general | solution.py:72
  215.0 3.5 %fusion.30 = f32[2,32,12,384]{3,1,2,0:T(8,128)} fusion(bf16[2,32,384,12]{2,1,3,0:T(8,128)(2,1)S(1)} %copy.25), kind=kOutput, calls=%fused_computation.48 | convolution fusion | flops 228114432 | bytes 1769472 | tf_op jit(solution)/shard_map/cxky,kz->cxyz/dot_general | solution.py:72
  218.6 0.0 copy-done
  218.6 1.6 copy.26
  220.2 2.0 copy.27
  222.2 0.0 copy-start.1
  222.2 3.9 %convolution_subtract_fusion = f32[2,32,12,384]{3,1,2,0:T(8,128)S(1)} fusion(f32[2,32,12,384]{3,1,2,0:T(8,128)} %fusion.34, bf16[2,32,384,12]{2,1,3,0:T(8,128)(2,1)S(1)} %copy.27), kind=kOutput, calls=%fused_computation.18 | convolution fusion | flops 228409344 | bytes 2949120 | tf_op jit(solution)/shard_map/cxky,kz->cxyz/dot_general | solution.py:72
  226.1 0.0 copy-done.1
  226.1 4.8 %add_reduce_fusion = (f32[32,12,384]{2,0,1:T(8,128)S(1)}, f32[32,12,384]{2,0,1:T(8,128)S(1)}) fusion(f32[2,32,12,384]{3,1,2,0:T(8,128)S(1)} %convolution_subtract_fusion, f32[2,2,32,12,384]{4,2,3,1,0:T(8,128)S(1)} %copy-done.1, f32[2,32,12,384]{3,1,2,0:T(8,128)} %fusion.30, bf16[2,32,384,12]{2,1,3,0:T(8,128)(2,1)S(1)} %copy.27), kind=kOutput, calls=%fused_computation.30 | convolution fusion | flops 230473728 | bytes 6488064 | tf_op jit(solution)/shard_map/cxky,kz->cxyz/dot_general | solution.py:72
  230.9 0.3 stack.24
  231.3 0.6 copy.30
  231.9 0.3 stack.25
  232.2 0.6 copy.31
  232.9 1.1 pad_maximum_fusion.1
  233.9 73.3 %all_to_all.20 = f32[16,2,2,12,384]{4,2,3,1,0:T(2,128)S(1)} all-to-all(f32[16,2,2,12,384]{4,2,3,1,0:T(2,128)S(1)} %pad_maximum_fusion.1), channel_id=1, replica_groups=mesh['coil'=16,'slab'=32] {'coil'}, dimensions={0} | all-to-all | bytes 2359296 | tf_op jit(solution)/shard_map/all_to_all | solution.py:20
  307.2 1.0 reduce_sum.29
Async XLA Ops:
  116.0 15.0 %copy-start.2 = (bf16[2,2,32,12,384]{4,2,3,1,0:T(8,128)(2,1)S(1)}, bf16[2,2,32,12,384]{4,2,3,1,0:T(8,128)(2,1)}, u32[]{:S(2)}) copy-start(bf16[2,2,32,12,384]{4,2,3,1,0:T(8,128)(2,1)} %param.8) | copy-start | bytes 3538948
  116.0 71.4 %all-to-all-start = ((bf16[32,2,9216]{2,1,0:T(2,128)(2,1)}), bf16[32,2,9216]{2,1,0:T(2,128)(2,1)S(1)}, u32[]{:S(2)}, u32[]{:S(2)}) async-start(bf16[32,2,9216]{2,1,0:T(2,128)(2,1)} %reshape.84), calls=%async_computation | async-start | bytes 2359296 | tf_op jit(solution)/shard_map/all_to_all | solution.py:93
  211.4 7.2 %copy-start = (bf16[1,2,32,32,12,12]{2,1,5,3,4,0:T(2,128)(2,1)S(1)}, bf16[1,2,32,32,12,12]{2,1,5,3,4,0:T(2,128)(2,1)}, u32[]{:S(2)}) copy-start(bf16[1,2,32,32,12,12]{2,1,5,3,4,0:T(2,128)(2,1)} %get-tuple-element.31) | copy-start | bytes 1769476
  222.2 4.0 %copy-start.1 = (f32[2,2,32,12,384]{4,2,3,1,0:T(8,128)S(1)}, f32[2,2,32,12,384]{4,2,3,1,0:T(8,128)}, u32[]{:S(2)}) copy-start(f32[2,2,32,12,384]{4,2,3,1,0:T(8,128)} %convert_element_type.32) | copy-start | bytes 7077892
where the time goes:
time: 309 us; the launch traced here: 308 us
  matrix products  110 us (36%)
  blocking collectives  73.3 us (24%)
  waiting for transfers between devices  54.7 us (18%)
  local copies, waits for them, and re-layouts  50.8 us (16%)
  starting transfers between devices  15 us (5%)
  other arithmetic  4.55 us (1%)
    dot_general x4, matrix products, lines_to_rows(): jnp.einsum('ctxkl,tkly->ctxky', left, right, preferred_element_type=jnp.f...  93.9 us
    all_to_all x1, blocking collectives, summed_on_arrival(): lax.all_to_all(blocks, axis, split_axis=0, concat_axis=0, tiled=True)  73.3 us
    all_to_all x1, waiting for transfers between devices, local(): lax.all_to_all(folded, 'slab', split_axis=4, concat_axis=3, tiled=True)  54.7 us
    dot_general x4, matrix products, along(): jnp.einsum('cxky,kz->cxyz', left, right, preferred_element_type=jnp.float32)  15.9 us
    unnamed x9, local copies, waits for them, and re-layouts  15.4 us
    all_to_all x1, starting transfers between devices, local(): lax.all_to_all(folded, 'slab', split_axis=4, concat_axis=3, tiled=True)  15 us
    slice x3, local copies, waits for them, and re-layouts, depth_pass(): image_real = along(harmonic[0], depth_cos) - along(harmonic[1], depth_sin)  10.3 us
    all_to_all x1, local copies, waits for them, and re-layouts, local(): lax.all_to_all(folded, 'slab', split_axis=4, concat_axis=3, tiled=True)  9.31 us
  transfers between devices with their start and end apart: 1, of which 1 were waited for; matrix products, arithmetic and copies ran while one was open for 1% of the time, Pallas kernels for 0%

commit v1 on v0

v1 whole, which is shorter than its diff:
```python
import functools
import math

import jax
import jax.numpy as jnp
import numpy as np
from jax import lax
from jax.experimental import pallas as pl
from jax.experimental.pallas import tpu as pltpu
from jax.sharding import PartitionSpec as P

NY = 384
NZ = 384
PHASES = 8
SLABS = 32
YL = NY // SLABS
KZL = NZ // SLABS
PAIRS = YL // 2
XR = 32
ROWS = KZL * 2
GROUPS = SLABS * PAIRS


def dft(rows, cols, length):
    turns = np.outer(rows, cols) % length
    angles = turns * (2.0 * math.pi / length)
    scaling = 1.0 / math.sqrt(length)
    return np.cos(angles) * scaling, np.sin(angles) * scaling


@functools.cache
def row_table():
    y = np.arange(SLABS)[:, None] * YL + np.arange(PAIRS)[None, :] * 2
    y = np.stack([y.reshape(-1), y.reshape(-1) + 1]).reshape(-1)
    cosine, sine = dft(y, np.arange(NY), NY)
    return np.concatenate([cosine, sine], axis=0).astype(jnp.bfloat16)


@functools.cache
def depth_table():
    cosine, sine = dft(np.arange(NZ), np.arange(NZ), NZ)
    from_real = np.concatenate([cosine, sine], axis=1)
    from_imag = np.concatenate([-sine, cosine], axis=1)
    return np.stack([from_real, from_imag], axis=1).reshape(2 * NZ, 2 * NZ).astype(jnp.bfloat16)


def encode_kernel(k_ref, line_ref, w_ref, out_ref, scratch):
    theta = 2.0 * math.pi / PHASES
    cosine = math.cos(theta)
    sine = math.sin(theta)
    ky = lax.broadcasted_iota(jnp.int32, (NY, 128), 0)
    low = lax.broadcasted_iota(jnp.int32, (GROUPS, 128), 1) < 64

    def grid_of(kz):
        first = jnp.concatenate([k_ref[r, c, 0, kz] for r in range(2) for c in range(2)], axis=0)
        later_re = jnp.concatenate([k_ref[0, c, 1, kz] for c in range(2)], axis=0).astype(jnp.float32)
        later_im = jnp.concatenate([k_ref[1, c, 1, kz] for c in range(2)], axis=0).astype(jnp.float32)
        later = jnp.concatenate(
            [cosine * later_re + sine * later_im, cosine * later_im - sine * later_re], axis=0
        ).astype(jnp.bfloat16)
        samples = jnp.concatenate([first, later], axis=1)
        chosen = jnp.concatenate(
            [jnp.where(ky == line_ref[kz, t : t + 1, :], 1.0, 0.0).astype(jnp.bfloat16) for t in range(2)],
            axis=1,
        )
        placed = lax.dot_general(
            chosen, samples, (((1,), (1,)), ((), ())), preferred_element_type=jnp.float32
        )
        return placed.astype(jnp.bfloat16)

    def split(a, b):
        swapped = pltpu.roll(jnp.where(low, b, a), 64, 1)
        return jnp.where(low, a, swapped), jnp.where(low, swapped, b)

    for pair in range(KZL // 2):
        grids = jnp.concatenate([grid_of(2 * pair), grid_of(2 * pair + 1)], axis=1)
        both = jnp.dot(w_ref[...], grids, preferred_element_type=jnp.float32)
        for half in range(2):
            kz = 2 * pair + half
            part = both[:, half * 128 : half * 128 + 128]
            cos_re, cos_im = split(part[:GROUPS], part[GROUPS : 2 * GROUPS])
            sin_re, sin_im = split(part[2 * GROUPS : 3 * GROUPS], part[3 * GROUPS :])
            scratch[pl.ds(2 * kz, GROUPS, stride=ROWS), :] = cos_re - sin_im
            scratch[pl.ds(2 * kz + 1, GROUPS, stride=ROWS), :] = sin_re + cos_im
    out_ref[...] = scratch[...].astype(jnp.bfloat16)


def encode(kspace, line_index):
    return pl.pallas_call(
        encode_kernel,
        out_shape=jax.ShapeDtypeStruct((GROUPS * ROWS, 128), jnp.bfloat16),
        in_specs=[pl.BlockSpec(memory_space=pltpu.VMEM)] * 3,
        out_specs=pl.BlockSpec(memory_space=pltpu.VMEM),
        scratch_shapes=[pltpu.VMEM((GROUPS * ROWS, 128), jnp.float32)],
        name="encode",
    )(jnp.transpose(kspace, (0, 1, 2, 4, 3, 5)), jnp.transpose(line_index, (1, 0, 2)), jnp.asarray(row_table()))


def image_kernel(r_ref, m_ref, d_ref, out_ref, scratch):
    for pair in range(PAIRS):
        arrived = r_ref[:, pair].astype(jnp.float32).reshape(SLABS * ROWS, 128)
        lhs = arrived.T.astype(jnp.bfloat16)
        image = jnp.dot(lhs, d_ref[...], preferred_element_type=jnp.float32)
        for which in range(2):
            y = 2 * pair + which
            real = None
            for c in range(2):
                start = which * 64 + c * 32
                image_re = image[start : start + 32, :NZ]
                image_im = image[start : start + 32, NZ:]
                map_re = m_ref[0, c, y].astype(jnp.float32)
                map_im = m_ref[1, c, y].astype(jnp.float32)
                add_re = map_re * image_re + map_im * image_im
                add_im = map_re * image_im - map_im * image_re
                real, imag = (add_re, add_im) if real is None else (real + add_re, imag + add_im)
            for part, value in enumerate((real, imag)):
                for lane in range(3):
                    scratch[lane, pl.ds(2 * y + part, XR, stride=ROWS), :] = value[:, lane * 128 : lane * 128 + 128]
    block = 2 * ROWS
    for xs in range(4):
        for zh in range(2):
            for core in range(2):
                src = (xs * 4 + zh * 2 + core) * block
                dst = (xs * 4 + core * 2 + zh) * block
                for lane in range(3):
                    out_ref[dst : dst + block, lane * 128 : lane * 128 + 128] = scratch[
                        lane, src : src + block, :
                    ].astype(jnp.bfloat16)


def images(arrived, coil_maps):
    return pl.pallas_call(
        image_kernel,
        out_shape=jax.ShapeDtypeStruct((XR * ROWS, NZ), jnp.bfloat16),
        in_specs=[pl.BlockSpec(memory_space=pltpu.VMEM)] * 3,
        out_specs=pl.BlockSpec(memory_space=pltpu.VMEM),
        scratch_shapes=[pltpu.VMEM((3, XR * ROWS, 128), jnp.float32)],
        name="images",
    )(
        arrived.reshape(SLABS, PAIRS, ROWS, 128),
        jnp.transpose(coil_maps, (0, 1, 3, 2, 4)),
        jnp.asarray(depth_table()),
    )


NEAR = [[x * 4 + far * 2 + core for x in range(4) for core in range(2)] for far in range(2)]
ACROSS = [(i, i ^ 2) for i in range(16)]


def combine(partial):
    arrived = lax.all_to_all(
        partial.reshape(8, 4 * ROWS, NZ), "coil", split_axis=0, concat_axis=0, tiled=True, axis_index_groups=NEAR
    )
    near = arrived.astype(jnp.float32).sum(axis=0).reshape(2, 2 * ROWS, NZ)
    far = (lax.axis_index("coil") // 2) % 2
    own = lax.dynamic_index_in_dim(near, far, 0, keepdims=False)
    other = lax.dynamic_index_in_dim(near, 1 - far, 0, keepdims=False)
    total = own + lax.ppermute(other, "coil", ACROSS)
    return jnp.transpose(total.reshape(2, YL, 2, NZ), (0, 2, 1, 3))


def local(kspace, coil_maps, line_index):
    sent = encode(kspace, line_index).reshape(SLABS, PAIRS * ROWS, 128)
    arrived = lax.all_to_all(sent, "slab", split_axis=0, concat_axis=0, tiled=True)
    return combine(images(arrived, coil_maps))


def solution(mesh):
    placed = (
        P(None, "coil", None, None, "slab", None),
        P(None, "coil", None, "slab", None),
        P(None, "slab", None),
    )
    return jax.shard_map(
        local, mesh=mesh, in_specs=placed, out_specs=P("coil", None, "slab", None), check_vma=False
    )
```

time: 309 us -> 119 us (0.39)
  the two profiles are of different devices: /device:TPU:33 before, /device:TPU:1 now
where the time goes in v1:
time: 119 us; the launch traced here: 118 us
  blocking collectives  73.5 us (62%)
  waiting for transfers between devices  20.2 us (17%)
  starting transfers between devices  14.3 us (12%)
  Pallas kernels  9.38 us (8%)
    all_to_all x1, blocking collectives, local(): lax.all_to_all(sent, 'slab', split_axis=0, concat_axis=0, tiled=True)  73.5 us
    ppermute x1, waiting for transfers between devices, combine(): total = own + lax.ppermute(other, 'coil', ACROSS)  10.1 us
    all_to_all x1, waiting for transfers between devices, combine(): lax.all_to_all(partial.reshape(8, 4 * ROWS, NZ), 'coil', split_axis=0, co...  10.1 us
    ppermute x1, starting transfers between devices, combine(): total = own + lax.ppermute(other, 'coil', ACROSS)  7.94 us
    all_to_all x1, starting transfers between devices, combine(): lax.all_to_all(partial.reshape(8, 4 * ROWS, NZ), 'coil', split_axis=0, co...  6.39 us
    pallas_call x1, Pallas kernels, encode(): pl.pallas_call(encode_kernel, out_shape=jax.ShapeDtypeStruct((GROUPS * RO...  5.16 us
    pallas_call x1, Pallas kernels, images(): pl.pallas_call(image_kernel, out_shape=jax.ShapeDtypeStruct((XR * ROWS, N...  4.22 us
  transfers between devices with their start and end apart: 2, of which 2 were waited for; matrix products, arithmetic and copies ran while one was open for 0% of the time, Pallas kernels for 0%

profile of v1, /device:TPU:1, one launch (start us, length us, event | category | flops | bytes accessed | tf_op | source)
XLA Modules:
  0.0 118.3 jit_solution(8227406375302117009)
XLA Ops:
  0.0 5.2 %encode.1 = bf16[4608,128]{1,0:T(8,128)(2,1)} custom-call(bf16[2,2,2,12,32,128]{5,4,3,2,1,0:T(8,128)(2,1)} %bitcast.16, s32[12,2,128]{2,1,0:T(2,128)} %bitcast.19, bf16[768,384]{1,0:T(8,128)(2,1)} %constant.45.clone.w_ref), custom_call_target="tpu_custom_call" | custom-call | tf_op jit(solution)/shard_map/encode/pallas_call | solution.py:89
  5.2 73.5 %all_to_all.10 = bf16[32,144,128]{2,1,0:T(8,128)(2,1)} all-to-all(bf16[32,144,128]{2,1,0:T(8,128)(2,1)} %bitcast.12), channel_id=1, replica_groups=mesh['coil'=16,'slab'=32] {'slab'}, dimensions={0} | all-to-all | bytes 2359296 | tf_op jit(solution)/shard_map/all_to_all | solution.py:164
  78.7 4.2 %images.1 = bf16[768,384]{1,0:T(8,128)(2,1)} custom-call(bf16[32,6,24,128]{3,2,1,0:T(8,128)(2,1)} %bitcast.13, bf16[2,2,12,32,384]{4,3,2,1,0:T(8,128)(2,1)} %bitcast.15, bf16[768,768]{1,0:T(8,128)(2,1)} %constant.46.clone.d_ref), custom_call_target="tpu_custom_call" | custom-call | tf_op jit(solution)/shard_map/images/pallas_call | solution.py:132
  82.9 6.4 %all-to-all-start.1 = ((bf16[8,96,384]{2,1,0:T(8,128)(2,1)}), bf16[8,96,384]{2,1,0:T(8,128)(2,1)S(1)}, u32[]{:S(2)}, u32[]{:S(2)}) async-start(bf16[8,96,384]{2,1,0:T(8,128)(2,1)} %bitcast.14), calls=%async_computation.1 | async-start | bytes 1179648 | tf_op jit(solution)/shard_map/all_to_all | solution.py:151
  89.3 10.1 %all-to-all-done.1 = bf16[8,96,384]{2,1,0:T(8,128)(2,1)S(1)} async-done(((bf16[8,96,384]{2,1,0:T(8,128)(2,1)}), bf16[8,96,384]{2,1,0:T(8,128)(2,1)S(1)}, u32[]{:S(2)}, u32[]{:S(2)}) %all-to-all-start.1) | async-done | bytes 589856 | tf_op jit(solution)/shard_map/all_to_all | solution.py:151
  99.4 0.1 convert_reduce_fusion
  99.5 7.9 %collective-permute-start = (f32[48,384]{1,0:T(8,128)S(1)}, f32[48,384]{1,0:T(8,128)S(1)}, u32[]{:S(2)}, u32[]{:S(2)}) collective-permute-start(f32[48,384]{1,0:T(8,128)S(1)} %dynamic-slice_bitcast_fusion), channel_id=1, source_target_pairs={{0,64},{32,96},{64,0},{96,32},{128,192},{160,224},{192,128},{224,1... | collective-permute-start | bytes 221192 | tf_op jit(solution)/shard_map/ppermute | solution.py:158
  107.4 10.1 %collective-permute-done = f32[48,384]{1,0:T(8,128)S(1)} collective-permute-done((f32[48,384]{1,0:T(8,128)S(1)}, f32[48,384]{1,0:T(8,128)S(1)}, u32[]{:S(2)}, u32[]{:S(2)}) %collective-permute-start) | collective-permute-done | bytes 73760 | tf_op jit(solution)/shard_map/ppermute | solution.py:158
  117.6 0.7 reshape.19
  (2 shorter events, 0.0 us)
Async XLA Ops:
  82.9 16.4 %all-to-all-start.1 = ((bf16[8,96,384]{2,1,0:T(8,128)(2,1)}), bf16[8,96,384]{2,1,0:T(8,128)(2,1)S(1)}, u32[]{:S(2)}, u32[]{:S(2)}) async-start(bf16[8,96,384]{2,1,0:T(8,128)(2,1)} %bitcast.14), calls=%async_computation.1 | async-start | bytes 1179648 | tf_op jit(solution)/shard_map/all_to_all | solution.py:151
  99.5 18.1 %collective-permute-start = (f32[48,384]{1,0:T(8,128)S(1)}, f32[48,384]{1,0:T(8,128)S(1)}, u32[]{:S(2)}, u32[]{:S(2)}) collective-permute-start(f32[48,384]{1,0:T(8,128)S(1)} %dynamic-slice_bitcast_fusion), channel_id=1, source_target_pairs={{0,64},{32,96},{64,0},{96,32},{128,192},{160,224},{192,128},{224,1... | collective-permute-start | bytes 221192 | tf_op jit(solution)/shard_map/ppermute | solution.py:158

commit v2 on v1

v2 whole, which is shorter than its diff:
```python
import functools
import math

import jax
import jax.numpy as jnp
import numpy as np
from jax import lax
from jax.experimental import pallas as pl
from jax.experimental.pallas import tpu as pltpu
from jax.sharding import Mesh
from jax.sharding import PartitionSpec as P

NY = 384
NZ = 384
PHASES = 8
SLABS = 32
YL = NY // SLABS
KZL = NZ // SLABS
CX = 4
XL = 8
BLOCK = 3 * KZL
SENT = CX * SLABS * BLOCK


def dft(rows, cols, length):
    turns = np.outer(rows, cols) % length
    angles = turns * (2.0 * math.pi / length)
    scaling = 1.0 / math.sqrt(length)
    return np.cos(angles) * scaling, np.sin(angles) * scaling


@functools.cache
def row_table():
    y = np.arange(YL)[:, None] + np.arange(SLABS)[None, :] * YL
    return np.concatenate(dft(y.reshape(-1), np.arange(NY), NY), axis=1).astype(jnp.bfloat16)


@functools.cache
def depth_table():
    kz = (np.arange(KZL)[:, None] + np.arange(SLABS)[None, :] * KZL).reshape(-1)
    cosine, sine = dft(kz, np.arange(NZ), NZ)
    from_real = np.concatenate([cosine, sine], axis=1)
    from_imag = np.concatenate([-sine, cosine], axis=1)
    return np.concatenate([from_real, from_imag], axis=0).astype(jnp.bfloat16)


def encode_kernel(k_ref, line_ref, w_ref, out_ref, scratch):
    theta = 2.0 * math.pi / PHASES
    cosine = math.cos(theta)
    sine = math.sin(theta)
    ky = lax.broadcasted_iota(jnp.int32, (NY, 128), 0)
    lanes = lax.broadcasted_iota(jnp.int32, (1, 128), 1)

    def grid_of(kz):
        early_re, early_im, late_re, late_im = (
            jnp.concatenate([k_ref[part, c, t, kz] for c in range(2)], axis=0)
            for t in range(2)
            for part in range(2)
        )
        late_re = late_re.astype(jnp.float32)
        late_im = late_im.astype(jnp.float32)
        turned_re = (cosine * late_re + sine * late_im).astype(jnp.bfloat16)
        turned_im = (cosine * late_im - sine * late_re).astype(jnp.bfloat16)
        early = jnp.concatenate([early_re, early_im, -early_im, early_re], axis=0)
        late = jnp.concatenate([turned_re, turned_im, -turned_im, turned_re], axis=0)
        samples = jnp.concatenate([early, late], axis=1)
        chosen = jnp.concatenate(
            [jnp.where(ky == line_ref[kz, t : t + 1, :], 1.0, 0.0).astype(jnp.bfloat16) for t in range(2)],
            axis=1,
        )
        placed = lax.dot_general(
            chosen, samples, (((1,), (1,)), ((), ())), preferred_element_type=jnp.float32
        ).astype(jnp.bfloat16)
        return jnp.concatenate([placed[:, :128], placed[:, 128:]], axis=0)

    def exchange(a, b, bit):
        upper = (lanes & bit) != 0
        return (
            jnp.where(upper, pltpu.roll(b, bit, 1), a),
            jnp.where(upper, b, pltpu.roll(a, 128 - bit, 1)),
        )

    for pair in range(KZL // 2):
        grids = jnp.concatenate([grid_of(2 * pair), grid_of(2 * pair + 1)], axis=1)
        both = jnp.dot(w_ref[...], grids, preferred_element_type=jnp.float32)
        for half in range(2):
            kz = 2 * pair + half
            for third in range(3):
                part = both[third * 128 : third * 128 + 128, half * 128 : half * 128 + 128]
                for high, sides in enumerate(exchange(part[:64], part[64:], 16)):
                    for low, value in enumerate(exchange(sides[:32], sides[32:], 8)):
                        start = (2 * high + low) * SLABS * BLOCK + third * KZL + kz
                        scratch[pl.ds(start, SLABS, stride=BLOCK), :] = value
    out_ref[...] = scratch[...].astype(jnp.bfloat16)


def encode(kspace, line_index):
    return pl.pallas_call(
        encode_kernel,
        out_shape=jax.ShapeDtypeStruct((SENT, 128), jnp.bfloat16),
        in_specs=[pl.BlockSpec(memory_space=pltpu.VMEM)] * 3,
        out_specs=pl.BlockSpec(memory_space=pltpu.VMEM),
        scratch_shapes=[pltpu.VMEM((SENT, 128), jnp.float32)],
        name="encode",
    )(jnp.transpose(kspace, (0, 1, 2, 4, 3, 5)), jnp.transpose(line_index, (1, 0, 2)), jnp.asarray(row_table()))


def image_kernel(me_ref, r_ref, m0_ref, m1_ref, m2_ref, m3_ref, d_ref, own_ref, other_ref, wide, lhs, sums):
    wide[...] = r_ref[...].astype(jnp.float32)
    column = me_ref[0]
    core = me_ref[1]
    for step in range(CX):
        base = (column ^ step) * (SLABS * BLOCK)
        for third in range(3):
            rows = jnp.concatenate(
                [wide[pl.ds(base + third * KZL + kz, SLABS, stride=BLOCK), :] for kz in range(KZL)], axis=0
            )
            turned = rows.T.astype(jnp.bfloat16)
            at = (step * 3 + third) * 64
            lhs[at : at + 64, : KZL * SLABS] = turned[:64]
            lhs[at : at + 64, KZL * SLABS :] = turned[64:]
    image = jnp.dot(lhs[...], d_ref[...], preferred_element_type=jnp.float32)
    for third in range(3):
        real = imag = None
        for step, m_ref in enumerate((m0_ref, m1_ref, m2_ref, m3_ref)):
            for c in range(2):
                at = (step * 3 + third) * 64 + c * 32
                image_re = image[at : at + 32, :NZ]
                image_im = image[at : at + 32, NZ:]
                map_re, map_im = (
                    m_ref[part, c, 4 * third : 4 * third + 4].astype(jnp.float32).reshape(32, NZ) for part in range(2)
                )
                add_re = map_re * image_re + map_im * image_im
                add_im = map_re * image_im - map_im * image_re
                real, imag = (add_re, add_im) if real is None else (real + add_re, imag + add_im)
        for part, value in enumerate((real, imag)):
            for y in range(4):
                for lane in range(3):
                    sums[lane, pl.ds(2 * (4 * third + y) + part, XL, stride=2 * YL), :] = value[
                        y * 8 : y * 8 + 8, lane * 128 : lane * 128 + 128
                    ]
    rows = 4 * YL
    for zh in range(2):
        for lane in range(3):
            at = slice(lane * 128, lane * 128 + 128)
            own_ref[zh * rows : zh * rows + rows, at] = sums[lane, pl.ds((2 * zh + core) * rows, rows), :]
            other_ref[zh * rows : zh * rows + rows, at] = sums[lane, pl.ds((2 * zh + 1 - core) * rows, rows), :]


def images(arrived, maps):
    me = jnp.stack([lax.axis_index("cx"), lax.axis_index("core")]).astype(jnp.int32)
    vmem = pl.BlockSpec(memory_space=pltpu.VMEM)
    half = jax.ShapeDtypeStruct((8 * YL, NZ), jnp.float32)
    return pl.pallas_call(
        image_kernel,
        out_shape=(half, half),
        in_specs=[pl.BlockSpec(memory_space=pltpu.SMEM)] + [vmem] * 6,
        out_specs=(vmem, vmem),
        scratch_shapes=[
            pltpu.VMEM((SENT, 128), jnp.float32),
            pltpu.VMEM((2 * NZ, 2 * NZ), jnp.bfloat16),
            pltpu.VMEM((3, 2 * YL * XL, 128), jnp.float32),
        ],
        name="images",
    )(me, arrived, *maps, jnp.asarray(depth_table()))


def shared_maps(coil_maps):
    rows = jnp.transpose(coil_maps, (0, 1, 3, 2, 4))
    column = lax.axis_index("cx")
    chunks = []
    for step in range(CX):
        chunk = lax.dynamic_slice_in_dim(rows, (column ^ step) * XL, XL, axis=3)
        if step:
            chunk = lax.ppermute(chunk, "cx", [(i, i ^ step) for i in range(CX)])
        chunks.append(chunk)
    return chunks


def local(kspace, coil_maps, line_index):
    sent, coil_maps = lax.optimization_barrier((encode(kspace, line_index), coil_maps))
    arrived = lax.all_to_all(
        sent.reshape(CX * SLABS, BLOCK // 4, 4, 128), ("cx", "slab"), split_axis=0, concat_axis=0, tiled=True
    ).reshape(SENT, 128)
    own, other = images(arrived, shared_maps(coil_maps))
    swap = [(0, 1), (1, 0)]
    pairs = (own + lax.ppermute(other, "core", swap)).reshape(2, 4 * YL, NZ)
    far = lax.axis_index("zh")
    own = lax.dynamic_index_in_dim(pairs, far, 0, keepdims=False)
    other = lax.dynamic_index_in_dim(pairs, 1 - far, 0, keepdims=False)
    total = own + lax.ppermute(other, "zh", swap)
    return jnp.transpose(total.reshape(2, YL, 2, NZ), (0, 2, 1, 3))


def solution(mesh):
    fine = Mesh(mesh.devices.reshape(CX, 2, 2, SLABS), ("cx", "zh", "core", "slab"))
    coil = ("cx", "zh", "core")
    placed = (
        P(None, coil, None, None, "slab", None),
        P(None, coil, None, "slab", None),
        P(None, "slab", None),
    )
    return jax.shard_map(
        local, mesh=fine, in_specs=placed, out_specs=P(coil, None, "slab", None), check_vma=False
    )
```

time: 119 us -> 113 us (0.950)
  blocking collectives: 73.5 us -> 0 us
  waiting for transfers between devices: 20.2 us -> 57.9 us
  starting transfers between devices: 14.3 us -> 41.7 us
  local copies, waits for them, and re-layouts: 0.69 us -> 2.56 us
  other arithmetic: 0.09 us -> 1.59 us
    all_to_all x1 -> x0, blocking collectives: 73.5 us -> none  [local(): lax.all_to_all(sent, 'slab', split_axis=0, concat_axis=0, tiled=True)]
    all_to_all x1, waiting for transfers between devices: 10.1 us -> 30.7 us  [local(): lax.all_to_all(sent.reshape(CX * SLABS, BLOCK // 4, 4, 128), ('cx', 'slab...]
    ppermute x1 -> x5, waiting for transfers between devices: 10.1 us -> 27.1 us  [the longest x3 17.3 us: shared_maps(): chunk = lax.ppermute(chunk, 'cx', [(i, i ^ step) for i in range(CX)])]
    all_to_all x1, starting transfers between devices: 6.39 us -> 20.5 us  [local(): lax.all_to_all(sent.reshape(CX * SLABS, BLOCK // 4, 4, 128), ('cx', 'slab...]
    ppermute x1 -> x5, starting transfers between devices: 7.94 us -> 21.2 us  [the longest x3 9.57 us: shared_maps(): chunk = lax.ppermute(chunk, 'cx', [(i, i ^ step) for i in range(CX)])]
  transfers between devices with their start and end apart: 2 -> 6, of which waited for: 2 -> 6; matrix products, arithmetic and copies ran while one was open for 0% -> 1% of each run, Pallas kernels for 0% -> 0%
where the time goes in v2:
time: 113 us
  waiting for transfers between devices  57.9 us (51%)
  starting transfers between devices  41.7 us (37%)
  Pallas kernels  9.26 us (8%)
  local copies, waits for them, and re-layouts  2.56 us (2%)
  other arithmetic  1.59 us (1%)
    all_to_all x1, waiting for transfers between devices, local(): lax.all_to_all(sent.reshape(CX * SLABS, BLOCK // 4, 4, 128), ('cx', 'slab...  30.7 us
    all_to_all x1, starting transfers between devices, local(): lax.all_to_all(sent.reshape(CX * SLABS, BLOCK // 4, 4, 128), ('cx', 'slab...  20.5 us
    ppermute x3, waiting for transfers between devices, shared_maps(): chunk = lax.ppermute(chunk, 'cx', [(i, i ^ step) for i in range(CX)])  17.3 us
    ppermute x3, starting transfers between devices, shared_maps(): chunk = lax.ppermute(chunk, 'cx', [(i, i ^ step) for i in range(CX)])  9.57 us
    ppermute x1, waiting for transfers between devices, local(): total = own + lax.ppermute(other, 'zh', swap)  8.63 us
    ppermute x1, starting transfers between devices, local(): total = own + lax.ppermute(other, 'zh', swap)  7.93 us
    pallas_call x1, Pallas kernels, encode(): pl.pallas_call(encode_kernel, out_shape=jax.ShapeDtypeStruct((SENT, 128),...  4.84 us
    pallas_call x1, Pallas kernels, images(): pl.pallas_call(image_kernel, out_shape=(half, half), in_specs=[pl.BlockSp...  4.41 us
  transfers between devices with their start and end apart: 6, of which 6 were waited for; matrix products, arithmetic and copies ran while one was open for 1% of the time, Pallas kernels for 0%

profile of v2, /device:TPU:1, one launch (start us, length us, event | category | flops | bytes accessed | tf_op | source)
XLA Modules:
  0.0 113.1 jit_solution(15653594775938108551)
XLA Ops:
  0.0 4.8 %encode.1 = bf16[4608,128]{1,0:T(8,128)(2,1)} custom-call(bf16[2,2,2,12,32,128]{5,4,3,2,1,0:T(8,128)(2,1)} %bitcast.22, s32[12,2,128]{2,1,0:T(2,128)} %bitcast.25, bf16[384,768]{1,0:T(8,128)(2,1)} %constant.39.clone.w_ref), custom_call_target="tpu_custom_call" | custom-call | tf_op jit(solution)/shard_map/encode/pallas_call | solution.py:98
  4.8 0.0 copy-start.1
  4.8 20.5 %all-to-all-start = ((bf16[128,9,4,128]{3,2,1,0:T(4,128)(2,1)}), bf16[128,9,4,128]{3,2,1,0:T(4,128)(2,1)S(1)}, u32[]{:S(2)}, u32[]{:S(2)}) async-start(bf16[128,9,4,128]{3,2,1,0:T(4,128)(2,1)} %bitcast.20), calls=%async_computation | async-start | bytes 2359296 | tf_op jit(solution)/shard_map/all_to_all | solution.py:182
  25.4 0.0 copy-done.1
  25.4 0.8 dynamic-slice_bitcast_fusion
  26.2 2.6 %collective-permute-start = (bf16[2,2,12,8,384]{4,3,2,1,0:T(8,128)(2,1)S(1)}, bf16[2,2,12,8,384]{4,3,2,1,0:T(8,128)(2,1)S(1)}, u32[]{:S(2)}, u32[]{:S(2)}) collective-permute-start(bf16[2,2,12,8,384]{4,3,2,1,0:T(8,128)(2,1)S(1)} %get-tuple-element.15), channel_id=1, source_target_pairs={{0,128},{128,0},{256,384},{384,256},{1,129},{129,1},{257,385},{385... | collective-permute-start | bytes 884744 | tf_op jit(solution)/shard_map/ppermute | solution.py:175
  28.8 4.7 %collective-permute-start.1 = (bf16[2,2,12,8,384]{4,3,2,1,0:T(8,128)(2,1)S(1)}, bf16[2,2,12,8,384]{4,3,2,1,0:T(8,128)(2,1)S(1)}, u32[]{:S(2)}, u32[]{:S(2)}) collective-permute-start(bf16[2,2,12,8,384]{4,3,2,1,0:T(8,128)(2,1)S(1)} %get-tuple-element.14), channel_id=1, source_target_pairs={{0,256},{128,384},{256,0},{384,128},{1,257},{129,385},{257,1},{385... | collective-permute-start | bytes 884744 | tf_op jit(solution)/shard_map/ppermute | solution.py:175
  33.6 2.3 %collective-permute-start.2 = (bf16[2,2,12,8,384]{4,3,2,1,0:T(8,128)(2,1)S(1)}, bf16[2,2,12,8,384]{4,3,2,1,0:T(8,128)(2,1)S(1)}, u32[]{:S(2)}, u32[]{:S(2)}) collective-permute-start(bf16[2,2,12,8,384]{4,3,2,1,0:T(8,128)(2,1)S(1)} %get-tuple-element.13), channel_id=1, source_target_pairs={{0,384},{128,256},{256,128},{384,0},{1,385},{129,257},{257,129},{3... | collective-permute-start | bytes 884744 | tf_op jit(solution)/shard_map/ppermute | solution.py:175
  35.8 0.6 pad_add_fusion.me_ref
  36.5 2.7 %collective-permute-done.m1_ref = bf16[2,2,12,8,384]{4,3,2,1,0:T(8,128)(2,1)S(1)} collective-permute-done((bf16[2,2,12,8,384]{4,3,2,1,0:T(8,128)(2,1)S(1)}, bf16[2,2,12,8,384]{4,3,2,1,0:T(8,128)(2,1)S(1)}, u32[]{:S(2)}, u32[]{:S(2)}) %collective-permute-start) | collective-permute-done | bytes 294944 | tf_op jit(solution)/shard_map/ppermute | solution.py:175
  39.2 0.0 copy-start.2
  39.2 9.8 %collective-permute-done.1.m2_ref = bf16[2,2,12,8,384]{4,3,2,1,0:T(8,128)(2,1)S(1)} collective-permute-done((bf16[2,2,12,8,384]{4,3,2,1,0:T(8,128)(2,1)S(1)}, bf16[2,2,12,8,384]{4,3,2,1,0:T(8,128)(2,1)S(1)}, u32[]{:S(2)}, u32[]{:S(2)}) %collective-permute-start.1) | collective-permute-done | bytes 294944 | tf_op jit(solution)/shard_map/ppermute | solution.py:175
  49.0 0.0 copy-start.3
  49.0 4.8 %collective-permute-done.2.m3_ref = bf16[2,2,12,8,384]{4,3,2,1,0:T(8,128)(2,1)S(1)} collective-permute-done((bf16[2,2,12,8,384]{4,3,2,1,0:T(8,128)(2,1)S(1)}, bf16[2,2,12,8,384]{4,3,2,1,0:T(8,128)(2,1)S(1)}, u32[]{:S(2)}, u32[]{:S(2)}) %collective-permute-start.2) | collective-permute-done | bytes 294944 | tf_op jit(solution)/shard_map/ppermute | solution.py:175
  53.8 0.0 copy-start.4
  53.8 30.7 %all-to-all-done = bf16[128,9,4,128]{3,2,1,0:T(4,128)(2,1)S(1)} async-done(((bf16[128,9,4,128]{3,2,1,0:T(4,128)(2,1)}), bf16[128,9,4,128]{3,2,1,0:T(4,128)(2,1)S(1)}, u32[]{:S(2)}, u32[]{:S(2)}) %all-to-all-start) | async-done | bytes 1179680 | tf_op jit(solution)/shard_map/all_to_all | solution.py:182
  84.5 0.0 copy-start
  84.5 0.0 copy-done.2
  84.5 0.0 copy-done.3
  84.5 0.0 copy-done.4
  84.6 1.0 copy-done
  85.6 4.4 %images.1 = (f32[96,384]{1,0:T(8,128)}, f32[96,384]{1,0:T(8,128)}) custom-call(s32[2]{0:T(128)} %pad_add_fusion.me_ref, bf16[4608,128]{1,0:T(8,128)(2,1)} %bitcast.21, bf16[2,2,12,8,384]{4,3,2,1,0:T(8,128)(2,1)} %get-tuple-element.16.m0_ref, bf16[2,2,12,8,384]{4,3,2,1,0:T(8,128)(2,1)} %copy-done.2, bf16[2,2,12,8,384]{4,3,2,1,0:T(8,128)(2,1)} %copy-done.3, ...), custom_call_target="tpu_custom_call" | custom-call | tf_op jit(solution)/shard_map/images/pallas_call | solution.py:154
  90.0 3.7 %collective-permute-start.3 = (f32[96,384]{1,0:T(8,128)}, f32[96,384]{1,0:T(8,128)S(1)}, u32[]{:S(2)}, u32[]{:S(2)}) collective-permute-start(f32[96,384]{1,0:T(8,128)} %get-tuple-element.12), channel_id=1, source_target_pairs={{0,32},{32,0},{1,33},{33,1},{2,34},{34,2},{3,35},{35,3},{4,36},{36... | collective-permute-start | bytes 442376 | tf_op jit(solution)/shard_map/ppermute | solution.py:187
  93.7 1.2 %collective-permute-done.3 = f32[96,384]{1,0:T(8,128)S(1)} collective-permute-done((f32[96,384]{1,0:T(8,128)}, f32[96,384]{1,0:T(8,128)S(1)}, u32[]{:S(2)}, u32[]{:S(2)}) %collective-permute-start.3) | collective-permute-done | bytes 147488 | tf_op jit(solution)/shard_map/ppermute | solution.py:187
  94.9 0.9 add.30
  95.8 7.9 %collective-permute-start.4 = (f32[48,384]{1,0:T(8,128)S(1)}, f32[48,384]{1,0:T(8,128)S(1)}, u32[]{:S(2)}, u32[]{:S(2)}) collective-permute-start(f32[48,384]{1,0:T(8,128)S(1)} %dynamic-slice_bitcast_fusion.4), channel_id=1, source_target_pairs={{0,64},{64,0},{1,65},{65,1},{2,66},{66,2},{3,67},{67,3},{4,68},{68... | collective-permute-start | bytes 221192 | tf_op jit(solution)/shard_map/ppermute | solution.py:191
  103.8 8.6 %collective-permute-done.4 = f32[48,384]{1,0:T(8,128)S(1)} collective-permute-done((f32[48,384]{1,0:T(8,128)S(1)}, f32[48,384]{1,0:T(8,128)S(1)}, u32[]{:S(2)}, u32[]{:S(2)}) %collective-permute-start.4) | collective-permute-done | bytes 73760 | tf_op jit(solution)/shard_map/ppermute | solution.py:191
  112.4 0.7 reshape.15
  (2 shorter events, 0.0 us)
Async XLA Ops:
  4.8 20.6 %copy-start.1 = (bf16[2,2,32,12,384]{4,2,3,1,0:T(8,128)(2,1)S(1)}, bf16[2,2,32,12,384]{4,2,3,1,0:T(8,128)(2,1)}, u32[]{:S(2)}) copy-start(bf16[2,2,32,12,384]{4,2,3,1,0:T(8,128)(2,1)} %param.6) | copy-start | bytes 3538948
  4.8 79.7 %all-to-all-start = ((bf16[128,9,4,128]{3,2,1,0:T(4,128)(2,1)}), bf16[128,9,4,128]{3,2,1,0:T(4,128)(2,1)S(1)}, u32[]{:S(2)}, u32[]{:S(2)}) async-start(bf16[128,9,4,128]{3,2,1,0:T(4,128)(2,1)} %bitcast.20), calls=%async_computation | async-start | bytes 2359296 | tf_op jit(solution)/shard_map/all_to_all | solution.py:182
  26.2 12.9 %collective-permute-start = (bf16[2,2,12,8,384]{4,3,2,1,0:T(8,128)(2,1)S(1)}, bf16[2,2,12,8,384]{4,3,2,1,0:T(8,128)(2,1)S(1)}, u32[]{:S(2)}, u32[]{:S(2)}) collective-permute-start(bf16[2,2,12,8,384]{4,3,2,1,0:T(8,128)(2,1)S(1)} %get-tuple-element.15), channel_id=1, source_target_pairs={{0,128},{128,0},{256,384},{384,256},{1,129},{129,1},{257,385},{385... | collective-permute-start | bytes 884744 | tf_op jit(solution)/shard_map/ppermute | solution.py:175
  28.8 20.2 %collective-permute-start.1 = (bf16[2,2,12,8,384]{4,3,2,1,0:T(8,128)(2,1)S(1)}, bf16[2,2,12,8,384]{4,3,2,1,0:T(8,128)(2,1)S(1)}, u32[]{:S(2)}, u32[]{:S(2)}) collective-permute-start(bf16[2,2,12,8,384]{4,3,2,1,0:T(8,128)(2,1)S(1)} %get-tuple-element.14), channel_id=1, source_target_pairs={{0,256},{128,384},{256,0},{384,128},{1,257},{129,385},{257,1},{385... | collective-permute-start | bytes 884744 | tf_op jit(solution)/shard_map/ppermute | solution.py:175
  33.6 20.3 %collective-permute-start.2 = (bf16[2,2,12,8,384]{4,3,2,1,0:T(8,128)(2,1)S(1)}, bf16[2,2,12,8,384]{4,3,2,1,0:T(8,128)(2,1)S(1)}, u32[]{:S(2)}, u32[]{:S(2)}) collective-permute-start(bf16[2,2,12,8,384]{4,3,2,1,0:T(8,128)(2,1)S(1)} %get-tuple-element.13), channel_id=1, source_target_pairs={{0,384},{128,256},{256,128},{384,0},{1,385},{129,257},{257,129},{3... | collective-permute-start | bytes 884744 | tf_op jit(solution)/shard_map/ppermute | solution.py:175
  39.2 45.4 %copy-start.2 = (bf16[2,2,12,8,384]{4,3,2,1,0:T(8,128)(2,1)}, bf16[2,2,12,8,384]{4,3,2,1,0:T(8,128)(2,1)S(1)}, u32[]{:S(2)}) copy-start(bf16[2,2,12,8,384]{4,3,2,1,0:T(8,128)(2,1)S(1)} %collective-permute-done.m1_ref) | copy-start | bytes 884740
  49.0 35.5 %copy-start.3 = (bf16[2,2,12,8,384]{4,3,2,1,0:T(8,128)(2,1)}, bf16[2,2,12,8,384]{4,3,2,1,0:T(8,128)(2,1)S(1)}, u32[]{:S(2)}) copy-start(bf16[2,2,12,8,384]{4,3,2,1,0:T(8,128)(2,1)S(1)} %collective-permute-done.1.m2_ref) | copy-start | bytes 884740
  53.8 30.7 %copy-start.4 = (bf16[2,2,12,8,384]{4,3,2,1,0:T(8,128)(2,1)}, bf16[2,2,12,8,384]{4,3,2,1,0:T(8,128)(2,1)S(1)}, u32[]{:S(2)}) copy-start(bf16[2,2,12,8,384]{4,3,2,1,0:T(8,128)(2,1)S(1)} %collective-permute-done.2.m3_ref) | copy-start | bytes 884740
  84.5 1.0 copy-start
  90.0 4.9 %collective-permute-start.3 = (f32[96,384]{1,0:T(8,128)}, f32[96,384]{1,0:T(8,128)S(1)}, u32[]{:S(2)}, u32[]{:S(2)}) collective-permute-start(f32[96,384]{1,0:T(8,128)} %get-tuple-element.12), channel_id=1, source_target_pairs={{0,32},{32,0},{1,33},{33,1},{2,34},{34,2},{3,35},{35,3},{4,36},{36... | collective-permute-start | bytes 442376 | tf_op jit(solution)/shard_map/ppermute | solution.py:187
  95.8 16.6 %collective-permute-start.4 = (f32[48,384]{1,0:T(8,128)S(1)}, f32[48,384]{1,0:T(8,128)S(1)}, u32[]{:S(2)}, u32[]{:S(2)}) collective-permute-start(f32[48,384]{1,0:T(8,128)S(1)} %dynamic-slice_bitcast_fusion.4), channel_id=1, source_target_pairs={{0,64},{64,0},{1,65},{65,1},{2,66},{66,2},{3,67},{67,3},{4,68},{68... | collective-permute-start | bytes 221192 | tf_op jit(solution)/shard_map/ppermute | solution.py:191

commit v3 on v2

--- a/solution.py
+++ b/solution.py
@@ -162,7 +162,7 @@
             pltpu.VMEM((3, 2 * YL * XL, 128), jnp.float32),
         ],
         name="images",
-    )(me, arrived, *maps, jnp.asarray(depth_table()))
+    )(me, *(pltpu.with_memory_space_constraint(x, pltpu.VMEM) for x in (arrived, *maps, jnp.asarray(depth_table()))))
 
 
 def shared_maps(coil_maps):
@@ -177,18 +177,22 @@
     return chunks
 
 
+def from_partner(value, axis):
+    pair = lax.all_gather(value, axis)
+    return lax.dynamic_index_in_dim(pair, 1 - lax.axis_index(axis), 0, keepdims=False)
+
+
 def local(kspace, coil_maps, line_index):
     sent, coil_maps = lax.optimization_barrier((encode(kspace, line_index), coil_maps))
     arrived = lax.all_to_all(
         sent.reshape(CX * SLABS, BLOCK // 4, 4, 128), ("cx", "slab"), split_axis=0, concat_axis=0, tiled=True
     ).reshape(SENT, 128)
     own, other = images(arrived, shared_maps(coil_maps))
-    swap = [(0, 1), (1, 0)]
-    pairs = (own + lax.ppermute(other, "core", swap)).reshape(2, 4 * YL, NZ)
+    pairs = (own + from_partner(other, "core")).reshape(2, 4 * YL, NZ)
     far = lax.axis_index("zh")
     own = lax.dynamic_index_in_dim(pairs, far, 0, keepdims=False)
     other = lax.dynamic_index_in_dim(pairs, 1 - far, 0, keepdims=False)
-    total = own + lax.ppermute(other, "zh", swap)
+    total = own + from_partner(other.astype(jnp.bfloat16), "zh").astype(jnp.float32)
     return jnp.transpose(total.reshape(2, YL, 2, NZ), (0, 2, 1, 3))
 
 

time: 113 us -> 106 us (0.938)
  blocking collectives: 0 us -> 16.2 us
  starting transfers between devices: 41.7 us -> 30 us
  waiting for transfers between devices: 57.9 us -> 46.6 us
  Pallas kernels: 9.26 us -> 7.93 us
    all_gather x0 -> x2, blocking collectives: none -> 16.2 us  [from_partner(): pair = lax.all_gather(value, axis)]
    ppermute x2 -> x0, starting transfers between devices: 11.6 us -> none  [the longest x1 7.93 us: local(): total = own + lax.ppermute(other, 'zh', swap)]
    ppermute x2 -> x0, waiting for transfers between devices: 9.82 us -> none  [the longest x1 8.63 us: local(): total = own + lax.ppermute(other, 'zh', swap)]
    all_to_all x1, waiting for transfers between devices: 30.7 us -> 28.3 us  [local(): lax.all_to_all(sent.reshape(CX * SLABS, BLOCK // 4, 4, 128), ('cx', 'slab...]
    dynamic_slice x1, local copies, waits for them, and re-layouts: 0.84 us -> 2.32 us  [shared_maps(): chunk = lax.dynamic_slice_in_dim(rows, (column ^ step) * XL, XL, axis=3)]
    pallas_call x1, Pallas kernels: 4.41 us -> 3.09 us  [images(): pl.pallas_call(image_kernel, out_shape=(half, half), in_specs=[pl.BlockSp...]
  transfers between devices with their start and end apart: 6 -> 4, of which waited for: 6 -> 4; matrix products, arithmetic and copies ran while one was open for 1% -> 3% of each run, Pallas kernels for 0% -> 0%
where the time goes in v3:
time: 106 us; the launch traced here: 105 us
  waiting for transfers between devices  46.6 us (44%)
  starting transfers between devices  30 us (28%)
  blocking collectives  16.2 us (15%)
  Pallas kernels  7.93 us (7%)
  local copies, waits for them, and re-layouts  3.02 us (3%)
  other arithmetic  1.52 us (1%)
    all_to_all x1, waiting for transfers between devices, local(): lax.all_to_all(sent.reshape(CX * SLABS, BLOCK // 4, 4, 128), ('cx', 'slab...  28.3 us
    all_to_all x1, starting transfers between devices, local(): lax.all_to_all(sent.reshape(CX * SLABS, BLOCK // 4, 4, 128), ('cx', 'slab...  20.4 us
    ppermute x3, waiting for transfers between devices, shared_maps(): chunk = lax.ppermute(chunk, 'cx', [(i, i ^ step) for i in range(CX)])  18.3 us
    all_gather x2, blocking collectives, from_partner(): pair = lax.all_gather(value, axis)  16.2 us
    ppermute x3, starting transfers between devices, shared_maps(): chunk = lax.ppermute(chunk, 'cx', [(i, i ^ step) for i in range(CX)])  9.57 us
    pallas_call x1, Pallas kernels, encode(): pl.pallas_call(encode_kernel, out_shape=jax.ShapeDtypeStruct((SENT, 128),...  4.84 us
    pallas_call x1, Pallas kernels, images(): pl.pallas_call(image_kernel, out_shape=(half, half), in_specs=[pl.BlockSp...  3.09 us
    dynamic_slice x1, local copies, waits for them, and re-layouts, shared_maps(): chunk = lax.dynamic_slice_in_dim(rows, (column ^ step) * XL, XL, axis=3)  2.32 us
  transfers between devices with their start and end apart: 4, of which 4 were waited for; matrix products, arithmetic and copies ran while one was open for 3% of the time, Pallas kernels for 0%

profile of v3, /device:TPU:1, one launch (start us, length us, event | category | flops | bytes accessed | tf_op | source)
XLA Modules:
  0.0 105.4 jit_solution(8170923310684788276)
XLA Ops:
  0.0 4.8 %encode.1 = bf16[4608,128]{1,0:T(8,128)(2,1)} custom-call(bf16[2,2,2,12,32,128]{5,4,3,2,1,0:T(8,128)(2,1)} %bitcast.21, s32[12,2,128]{2,1,0:T(2,128)} %bitcast.25, bf16[384,768]{1,0:T(8,128)(2,1)} %constant.48.clone.w_ref), custom_call_target="tpu_custom_call" | custom-call | tf_op jit(solution)/shard_map/encode/pallas_call | solution.py:98
  4.8 20.4 %all-to-all-start = ((bf16[128,9,4,128]{3,2,1,0:T(4,128)(2,1)}), bf16[128,9,4,128]{3,2,1,0:T(4,128)(2,1)S(1)}, u32[]{:S(2)}, u32[]{:S(2)}) async-start(bf16[128,9,4,128]{3,2,1,0:T(4,128)(2,1)} %bitcast.20), calls=%async_computation | async-start | bytes 2359296 | tf_op jit(solution)/shard_map/all_to_all | solution.py:187
  25.3 0.0 copy-start
  25.3 2.3 %dynamic-slice_bitcast_fusion = (bf16[2,2,12,8,384]{4,3,2,1,0:T(8,128)(2,1)}, bf16[2,2,12,8,384]{4,3,2,1,0:T(8,128)(2,1)}, bf16[2,2,12,8,384]{4,3,2,1,0:T(8,128)(2,1)}, bf16[2,2,12,8,384]{4,3,2,1,0:T(8,128)(2,1)S(1)}) fusion(bf16[2,2,32,12,384]{4,2,3,1,0:T(8,128)(2,1)} %param.6, s32[]{:T(128)S(6)} %select_n.28, s32[]{:T(128)S(6)} %select_n.27, ...), kind=kLoop, calls=%fused_computation | loop fusion | bytes 2359312 | tf_op jit(solution)/shard_map/dynamic_slice | solution.py:173
  27.6 2.6 %collective-permute-start = (bf16[2,2,12,8,384]{4,3,2,1,0:T(8,128)(2,1)}, bf16[2,2,12,8,384]{4,3,2,1,0:T(8,128)(2,1)S(1)}, u32[]{:S(2)}, u32[]{:S(2)}) collective-permute-start(bf16[2,2,12,8,384]{4,3,2,1,0:T(8,128)(2,1)} %get-tuple-element.15), channel_id=1, source_target_pairs={{0,128},{128,0},{256,384},{384,256},{1,129},{129,1},{257,385},{385... | collective-permute-start | bytes 884744 | tf_op jit(solution)/shard_map/ppermute | solution.py:175
  30.2 4.7 %collective-permute-start.1 = (bf16[2,2,12,8,384]{4,3,2,1,0:T(8,128)(2,1)}, bf16[2,2,12,8,384]{4,3,2,1,0:T(8,128)(2,1)S(1)}, u32[]{:S(2)}, u32[]{:S(2)}) collective-permute-start(bf16[2,2,12,8,384]{4,3,2,1,0:T(8,128)(2,1)} %get-tuple-element.14), channel_id=1, source_target_pairs={{0,256},{128,384},{256,0},{384,128},{1,257},{129,385},{257,1},{385... | collective-permute-start | bytes 884744 | tf_op jit(solution)/shard_map/ppermute | solution.py:175
  34.9 2.3 %collective-permute-start.2 = (bf16[2,2,12,8,384]{4,3,2,1,0:T(8,128)(2,1)}, bf16[2,2,12,8,384]{4,3,2,1,0:T(8,128)(2,1)S(1)}, u32[]{:S(2)}, u32[]{:S(2)}) collective-permute-start(bf16[2,2,12,8,384]{4,3,2,1,0:T(8,128)(2,1)} %get-tuple-element.13), channel_id=1, source_target_pairs={{0,384},{128,256},{256,128},{384,0},{1,385},{129,257},{257,129},{3... | collective-permute-start | bytes 884744 | tf_op jit(solution)/shard_map/ppermute | solution.py:175
  37.2 0.6 pad_add_fusion.me_ref
  37.8 2.2 %collective-permute-done.m1_ref = bf16[2,2,12,8,384]{4,3,2,1,0:T(8,128)(2,1)S(1)} collective-permute-done((bf16[2,2,12,8,384]{4,3,2,1,0:T(8,128)(2,1)}, bf16[2,2,12,8,384]{4,3,2,1,0:T(8,128)(2,1)S(1)}, u32[]{:S(2)}, u32[]{:S(2)}) %collective-permute-start) | collective-permute-done | bytes 294944 | tf_op jit(solution)/shard_map/ppermute | solution.py:175
  40.0 9.5 %collective-permute-done.1.m2_ref = bf16[2,2,12,8,384]{4,3,2,1,0:T(8,128)(2,1)S(1)} collective-permute-done((bf16[2,2,12,8,384]{4,3,2,1,0:T(8,128)(2,1)}, bf16[2,2,12,8,384]{4,3,2,1,0:T(8,128)(2,1)S(1)}, u32[]{:S(2)}, u32[]{:S(2)}) %collective-permute-start.1) | collective-permute-done | bytes 294944 | tf_op jit(solution)/shard_map/ppermute | solution.py:175
  49.4 6.6 %collective-permute-done.2.m3_ref = bf16[2,2,12,8,384]{4,3,2,1,0:T(8,128)(2,1)S(1)} collective-permute-done((bf16[2,2,12,8,384]{4,3,2,1,0:T(8,128)(2,1)}, bf16[2,2,12,8,384]{4,3,2,1,0:T(8,128)(2,1)S(1)}, u32[]{:S(2)}, u32[]{:S(2)}) %collective-permute-start.2) | collective-permute-done | bytes 294944 | tf_op jit(solution)/shard_map/ppermute | solution.py:175
  56.1 28.3 %all-to-all-done = bf16[128,9,4,128]{3,2,1,0:T(4,128)(2,1)S(1)} async-done(((bf16[128,9,4,128]{3,2,1,0:T(4,128)(2,1)}), bf16[128,9,4,128]{3,2,1,0:T(4,128)(2,1)S(1)}, u32[]{:S(2)}, u32[]{:S(2)}) %all-to-all-start) | async-done | bytes 1179680 | tf_op jit(solution)/shard_map/all_to_all | solution.py:187
  84.4 0.0 copy-done
  84.4 3.1 %images.1 = (f32[96,384]{1,0:T(8,128)}, f32[96,384]{1,0:T(8,128)}) custom-call(s32[2]{0:T(128)} %pad_add_fusion.me_ref, bf16[4608,128]{1,0:T(8,128)(2,1)S(1)} %bitcast.19, bf16[2,2,12,8,384]{4,3,2,1,0:T(8,128)(2,1)S(1)} %get-tuple-element.16.m0_ref, bf16[2,2,12,8,384]{4,3,2,1,0:T(8,128)(2,1)S(1)} %collective-permute-done.m1_ref, ...), custom_call_target="tpu_custom_call" | custom-call | tf_op jit(solution)/shard_map/images/pallas_call | solution.py:154
  87.5 3.6 %all-gather = f32[192,384]{1,0:T(8,128)S(1)} all-gather(f32[96,384]{1,0:T(8,128)} %get-tuple-element.12), channel_id=2, replica_groups=mesh['cx'=4,'zh'=2,'core'=2,'slab'=32] {'core'}, dimensions={0}, use_global_device_ids=true | all-gather | bytes 442368 | tf_op jit(solution)/shard_map/all_gather | solution.py:181
  91.1 0.9 bitcast_add_fusion
  92.1 12.6 %all_gather.12 = bf16[2,48,384]{2,1,0:T(8,128)(2,1)S(1)} all-gather(bf16[1,48,384]{2,1,0:T(8,128)(2,1)S(1)} %dynamic-slice_convert_fusion), channel_id=1, replica_groups=mesh['cx'=4,'zh'=2,'core'=2,'slab'=32] {'zh'}, dimensions={0}, use_global_device_ids=true | all-gather | bytes 110592 | tf_op jit(solution)/shard_map/all_gather | solution.py:181
  104.7 0.7 add.46
  (2 shorter events, 0.0 us)
Async XLA Ops:
  4.8 79.6 %all-to-all-start = ((bf16[128,9,4,128]{3,2,1,0:T(4,128)(2,1)}), bf16[128,9,4,128]{3,2,1,0:T(4,128)(2,1)S(1)}, u32[]{:S(2)}, u32[]{:S(2)}) async-start(bf16[128,9,4,128]{3,2,1,0:T(4,128)(2,1)} %bitcast.20), calls=%async_computation | async-start | bytes 2359296 | tf_op jit(solution)/shard_map/all_to_all | solution.py:187
  25.3 59.1 %copy-start = (bf16[768,768]{1,0:T(8,128)(2,1)S(1)}, bf16[768,768]{1,0:T(8,128)(2,1)}, u32[]{:S(2)}) copy-start(bf16[768,768]{1,0:T(8,128)(2,1)} %constant.49.clone.d_ref) | copy-start | bytes 3538948
  27.6 12.4 %collective-permute-start = (bf16[2,2,12,8,384]{4,3,2,1,0:T(8,128)(2,1)}, bf16[2,2,12,8,384]{4,3,2,1,0:T(8,128)(2,1)S(1)}, u32[]{:S(2)}, u32[]{:S(2)}) collective-permute-start(bf16[2,2,12,8,384]{4,3,2,1,0:T(8,128)(2,1)} %get-tuple-element.15), channel_id=1, source_target_pairs={{0,128},{128,0},{256,384},{384,256},{1,129},{129,1},{257,385},{385... | collective-permute-start | bytes 884744 | tf_op jit(solution)/shard_map/ppermute | solution.py:175
  30.2 19.3 %collective-permute-start.1 = (bf16[2,2,12,8,384]{4,3,2,1,0:T(8,128)(2,1)}, bf16[2,2,12,8,384]{4,3,2,1,0:T(8,128)(2,1)S(1)}, u32[]{:S(2)}, u32[]{:S(2)}) collective-permute-start(bf16[2,2,12,8,384]{4,3,2,1,0:T(8,128)(2,1)} %get-tuple-element.14), channel_id=1, source_target_pairs={{0,256},{128,384},{256,0},{384,128},{1,257},{129,385},{257,1},{385... | collective-permute-start | bytes 884744 | tf_op jit(solution)/shard_map/ppermute | solution.py:175
  34.9 21.1 %collective-permute-start.2 = (bf16[2,2,12,8,384]{4,3,2,1,0:T(8,128)(2,1)}, bf16[2,2,12,8,384]{4,3,2,1,0:T(8,128)(2,1)S(1)}, u32[]{:S(2)}, u32[]{:S(2)}) collective-permute-start(bf16[2,2,12,8,384]{4,3,2,1,0:T(8,128)(2,1)} %get-tuple-element.13), channel_id=1, source_target_pairs={{0,384},{128,256},{256,128},{384,0},{1,385},{129,257},{257,129},{3... | collective-permute-start | bytes 884744 | tf_op jit(solution)/shard_map/ppermute | solution.py:175

commit v4 on v3

--- a/solution.py
+++ b/solution.py
@@ -86,11 +86,11 @@
         for half in range(2):
             kz = 2 * pair + half
             for third in range(3):
-                part = both[third * 128 : third * 128 + 128, half * 128 : half * 128 + 128]
+                part = both[third * 128 : third * 128 + 128, half * 128 : half * 128 + 128].astype(jnp.bfloat16)
                 for high, sides in enumerate(exchange(part[:64], part[64:], 16)):
                     for low, value in enumerate(exchange(sides[:32], sides[32:], 8)):
                         start = (2 * high + low) * SLABS * BLOCK + third * KZL + kz
-                        scratch[pl.ds(start, SLABS, stride=BLOCK), :] = value
+                        scratch[pl.ds(start, SLABS, stride=BLOCK), :] = value.astype(jnp.float32)
     out_ref[...] = scratch[...].astype(jnp.bfloat16)
 
 
@@ -109,22 +109,20 @@
     wide[...] = r_ref[...].astype(jnp.float32)
     column = me_ref[0]
     core = me_ref[1]
-    for step in range(CX):
-        base = (column ^ step) * (SLABS * BLOCK)
-        for third in range(3):
+    for third in range(3):
+        for step in range(CX):
+            base = (column ^ step) * (SLABS * BLOCK)
             rows = jnp.concatenate(
                 [wide[pl.ds(base + third * KZL + kz, SLABS, stride=BLOCK), :] for kz in range(KZL)], axis=0
             )
             turned = rows.T.astype(jnp.bfloat16)
-            at = (step * 3 + third) * 64
-            lhs[at : at + 64, : KZL * SLABS] = turned[:64]
-            lhs[at : at + 64, KZL * SLABS :] = turned[64:]
-    image = jnp.dot(lhs[...], d_ref[...], preferred_element_type=jnp.float32)
-    for third in range(3):
+            lhs[third, step * 64 : step * 64 + 64, : KZL * SLABS] = turned[:64]
+            lhs[third, step * 64 : step * 64 + 64, KZL * SLABS :] = turned[64:]
+        image = jnp.dot(lhs[third], d_ref[...], preferred_element_type=jnp.float32)
         real = imag = None
         for step, m_ref in enumerate((m0_ref, m1_ref, m2_ref, m3_ref)):
             for c in range(2):
-                at = (step * 3 + third) * 64 + c * 32
+                at = step * 64 + c * 32
                 image_re = image[at : at + 32, :NZ]
                 image_im = image[at : at + 32, NZ:]
                 map_re, map_im = (
@@ -158,9 +156,10 @@
         out_specs=(vmem, vmem),
         scratch_shapes=[
             pltpu.VMEM((SENT, 128), jnp.float32),
-            pltpu.VMEM((2 * NZ, 2 * NZ), jnp.bfloat16),
+            pltpu.VMEM((3, 4 * 64, 2 * NZ), jnp.bfloat16),
             pltpu.VMEM((3, 2 * YL * XL, 128), jnp.float32),
         ],
+        compiler_params=pltpu.CompilerParams(vmem_limit_bytes=24 << 20),
         name="images",
     )(me, *(pltpu.with_memory_space_constraint(x, pltpu.VMEM) for x in (arrived, *maps, jnp.asarray(depth_table()))))
 

time: 106 us -> 103 us (0.972)
  other arithmetic: 1.52 us -> 0.1 us
  Pallas kernels: 7.93 us -> 6.69 us
  transfers between devices with their start and end apart: 4 -> 4, of which waited for: 4 -> 4; matrix products, arithmetic and copies ran while one was open for 3% -> 2% of each run, Pallas kernels for 0% -> 0%
where the time goes in v4:
time: 103 us
  waiting for transfers between devices  47.1 us (46%)
  starting transfers between devices  30 us (29%)
  blocking collectives  16 us (16%)
  Pallas kernels  6.69 us (6%)
  local copies, waits for them, and re-layouts  3.02 us (3%)
    all_to_all x1, waiting for transfers between devices, local(): lax.all_to_all(sent.reshape(CX * SLABS, BLOCK // 4, 4, 128), ('cx', 'slab...  28.3 us
    all_to_all x1, starting transfers between devices, local(): lax.all_to_all(sent.reshape(CX * SLABS, BLOCK // 4, 4, 128), ('cx', 'slab...  20.4 us
    ppermute x3, waiting for transfers between devices, shared_maps(): chunk = lax.ppermute(chunk, 'cx', [(i, i ^ step) for i in range(CX)])  18.8 us
    all_gather x2, blocking collectives, from_partner(): pair = lax.all_gather(value, axis)  16 us
    ppermute x3, starting transfers between devices, shared_maps(): chunk = lax.ppermute(chunk, 'cx', [(i, i ^ step) for i in range(CX)])  9.57 us
    pallas_call x1, Pallas kernels, encode(): pl.pallas_call(encode_kernel, out_shape=jax.ShapeDtypeStruct((SENT, 128),...  4.62 us
    dynamic_slice x1, local copies, waits for them, and re-layouts, shared_maps(): chunk = lax.dynamic_slice_in_dim(rows, (column ^ step) * XL, XL, axis=3)  2.32 us
    pallas_call x1, Pallas kernels, images(): pl.pallas_call(image_kernel, out_shape=(half, half), in_specs=[pl.BlockSp...  2.08 us
  transfers between devices with their start and end apart: 4, of which 4 were waited for; matrix products, arithmetic and copies ran while one was open for 2% of the time, Pallas kernels for 0%

profile of v4, /device:TPU:1, one launch (start us, length us, event | category | flops | bytes accessed | tf_op | source)
XLA Modules:
  0.0 103.0 jit_solution(386643011422189818)
XLA Ops:
  0.0 4.6 %encode.1 = bf16[4608,128]{1,0:T(8,128)(2,1)} custom-call(bf16[2,2,2,12,32,128]{5,4,3,2,1,0:T(8,128)(2,1)} %bitcast.21, s32[12,2,128]{2,1,0:T(2,128)} %bitcast.25, bf16[384,768]{1,0:T(8,128)(2,1)} %constant.48.clone.w_ref), custom_call_target="tpu_custom_call" | custom-call | tf_op jit(solution)/shard_map/encode/pallas_call | solution.py:98
  4.6 20.4 %all-to-all-start = ((bf16[128,9,4,128]{3,2,1,0:T(4,128)(2,1)}), bf16[128,9,4,128]{3,2,1,0:T(4,128)(2,1)S(1)}, u32[]{:S(2)}, u32[]{:S(2)}) async-start(bf16[128,9,4,128]{3,2,1,0:T(4,128)(2,1)} %bitcast.20), calls=%async_computation | async-start | bytes 2359296 | tf_op jit(solution)/shard_map/all_to_all | solution.py:186
  25.0 0.0 copy-start
  25.1 2.3 %dynamic-slice_bitcast_fusion = (bf16[2,2,12,8,384]{4,3,2,1,0:T(8,128)(2,1)}, bf16[2,2,12,8,384]{4,3,2,1,0:T(8,128)(2,1)}, bf16[2,2,12,8,384]{4,3,2,1,0:T(8,128)(2,1)}, bf16[2,2,12,8,384]{4,3,2,1,0:T(8,128)(2,1)S(1)}) fusion(bf16[2,2,32,12,384]{4,2,3,1,0:T(8,128)(2,1)} %param.6, s32[]{:T(128)S(6)} %select_n.28, s32[]{:T(128)S(6)} %select_n.27, ...), kind=kLoop, calls=%fused_computation | loop fusion | bytes 2359312 | tf_op jit(solution)/shard_map/dynamic_slice | solution.py:172
  27.4 2.6 %collective-permute-start = (bf16[2,2,12,8,384]{4,3,2,1,0:T(8,128)(2,1)}, bf16[2,2,12,8,384]{4,3,2,1,0:T(8,128)(2,1)S(1)}, u32[]{:S(2)}, u32[]{:S(2)}) collective-permute-start(bf16[2,2,12,8,384]{4,3,2,1,0:T(8,128)(2,1)} %get-tuple-element.15), channel_id=1, source_target_pairs={{0,128},{128,0},{256,384},{384,256},{1,129},{129,1},{257,385},{385... | collective-permute-start | bytes 884744 | tf_op jit(solution)/shard_map/ppermute | solution.py:174
  30.0 4.7 %collective-permute-start.1 = (bf16[2,2,12,8,384]{4,3,2,1,0:T(8,128)(2,1)}, bf16[2,2,12,8,384]{4,3,2,1,0:T(8,128)(2,1)S(1)}, u32[]{:S(2)}, u32[]{:S(2)}) collective-permute-start(bf16[2,2,12,8,384]{4,3,2,1,0:T(8,128)(2,1)} %get-tuple-element.14), channel_id=1, source_target_pairs={{0,256},{128,384},{256,0},{384,128},{1,257},{129,385},{257,1},{385... | collective-permute-start | bytes 884744 | tf_op jit(solution)/shard_map/ppermute | solution.py:174
  34.7 2.3 %collective-permute-start.2 = (bf16[2,2,12,8,384]{4,3,2,1,0:T(8,128)(2,1)}, bf16[2,2,12,8,384]{4,3,2,1,0:T(8,128)(2,1)S(1)}, u32[]{:S(2)}, u32[]{:S(2)}) collective-permute-start(bf16[2,2,12,8,384]{4,3,2,1,0:T(8,128)(2,1)} %get-tuple-element.13), channel_id=1, source_target_pairs={{0,384},{128,256},{256,128},{384,0},{1,385},{129,257},{257,129},{3... | collective-permute-start | bytes 884744 | tf_op jit(solution)/shard_map/ppermute | solution.py:174
  37.0 0.1 pad_add_fusion.me_ref
  37.1 2.7 %collective-permute-done.m1_ref = bf16[2,2,12,8,384]{4,3,2,1,0:T(8,128)(2,1)S(1)} collective-permute-done((bf16[2,2,12,8,384]{4,3,2,1,0:T(8,128)(2,1)}, bf16[2,2,12,8,384]{4,3,2,1,0:T(8,128)(2,1)S(1)}, u32[]{:S(2)}, u32[]{:S(2)}) %collective-permute-start) | collective-permute-done | bytes 294944 | tf_op jit(solution)/shard_map/ppermute | solution.py:174
  39.7 9.5 %collective-permute-done.1.m2_ref = bf16[2,2,12,8,384]{4,3,2,1,0:T(8,128)(2,1)S(1)} collective-permute-done((bf16[2,2,12,8,384]{4,3,2,1,0:T(8,128)(2,1)}, bf16[2,2,12,8,384]{4,3,2,1,0:T(8,128)(2,1)S(1)}, u32[]{:S(2)}, u32[]{:S(2)}) %collective-permute-start.1) | collective-permute-done | bytes 294944 | tf_op jit(solution)/shard_map/ppermute | solution.py:174
  49.2 6.6 %collective-permute-done.2.m3_ref = bf16[2,2,12,8,384]{4,3,2,1,0:T(8,128)(2,1)S(1)} collective-permute-done((bf16[2,2,12,8,384]{4,3,2,1,0:T(8,128)(2,1)}, bf16[2,2,12,8,384]{4,3,2,1,0:T(8,128)(2,1)S(1)}, u32[]{:S(2)}, u32[]{:S(2)}) %collective-permute-start.2) | collective-permute-done | bytes 294944 | tf_op jit(solution)/shard_map/ppermute | solution.py:174
  55.8 28.3 %all-to-all-done = bf16[128,9,4,128]{3,2,1,0:T(4,128)(2,1)S(1)} async-done(((bf16[128,9,4,128]{3,2,1,0:T(4,128)(2,1)}), bf16[128,9,4,128]{3,2,1,0:T(4,128)(2,1)S(1)}, u32[]{:S(2)}, u32[]{:S(2)}) %all-to-all-start) | async-done | bytes 1179680 | tf_op jit(solution)/shard_map/all_to_all | solution.py:186
  84.2 0.0 copy-done
  84.2 2.1 %images.1 = (f32[96,384]{1,0:T(8,128)S(1)}, f32[96,384]{1,0:T(8,128)S(1)}) custom-call(s32[2]{0:T(128)S(1)} %pad_add_fusion.me_ref, bf16[4608,128]{1,0:T(8,128)(2,1)S(1)} %bitcast.19, bf16[2,2,12,8,384]{4,3,2,1,0:T(8,128)(2,1)S(1)} %get-tuple-element.16.m0_ref, bf16[2,2,12,8,384]{4,3,2,1,0:T(8,128)(2,1)S(1)} %collective-permute-done.m1_ref, ...), custom_call_target="tpu_custom_call" | custom-call | tf_op jit(solution)/shard_map/images/pallas_call | solution.py:152
  86.3 3.4 %all-gather = f32[192,384]{1,0:T(8,128)S(1)} all-gather(f32[96,384]{1,0:T(8,128)S(1)} %get-tuple-element.12), channel_id=2, replica_groups=mesh['cx'=4,'zh'=2,'core'=2,'slab'=32] {'core'}, dimensions={0}, use_global_device_ids=true | all-gather | bytes 442368 | tf_op jit(solution)/shard_map/all_gather | solution.py:180
  89.8 12.6 %all_gather.12 = bf16[2,48,384]{2,1,0:T(8,128)(2,1)S(1)} all-gather(bf16[1,48,384]{2,1,0:T(8,128)(2,1)S(1)} %dynamic-slice_convert_fusion), channel_id=1, replica_groups=mesh['cx'=4,'zh'=2,'core'=2,'slab'=32] {'zh'}, dimensions={0}, use_global_device_ids=true | all-gather | bytes 110592 | tf_op jit(solution)/shard_map/all_gather | solution.py:180
  102.4 0.7 add.46
  (3 shorter events, 0.0 us)
Async XLA Ops:
  4.6 79.6 %all-to-all-start = ((bf16[128,9,4,128]{3,2,1,0:T(4,128)(2,1)}), bf16[128,9,4,128]{3,2,1,0:T(4,128)(2,1)S(1)}, u32[]{:S(2)}, u32[]{:S(2)}) async-start(bf16[128,9,4,128]{3,2,1,0:T(4,128)(2,1)} %bitcast.20), calls=%async_computation | async-start | bytes 2359296 | tf_op jit(solution)/shard_map/all_to_all | solution.py:186
  25.0 59.1 %copy-start = (bf16[768,768]{1,0:T(8,128)(2,1)S(1)}, bf16[768,768]{1,0:T(8,128)(2,1)}, u32[]{:S(2)}) copy-start(bf16[768,768]{1,0:T(8,128)(2,1)} %constant.49.clone.d_ref) | copy-start | bytes 3538948
  27.4 12.4 %collective-permute-start = (bf16[2,2,12,8,384]{4,3,2,1,0:T(8,128)(2,1)}, bf16[2,2,12,8,384]{4,3,2,1,0:T(8,128)(2,1)S(1)}, u32[]{:S(2)}, u32[]{:S(2)}) collective-permute-start(bf16[2,2,12,8,384]{4,3,2,1,0:T(8,128)(2,1)} %get-tuple-element.15), channel_id=1, source_target_pairs={{0,128},{128,0},{256,384},{384,256},{1,129},{129,1},{257,385},{385... | collective-permute-start | bytes 884744 | tf_op jit(solution)/shard_map/ppermute | solution.py:174
  30.0 19.3 %collective-permute-start.1 = (bf16[2,2,12,8,384]{4,3,2,1,0:T(8,128)(2,1)}, bf16[2,2,12,8,384]{4,3,2,1,0:T(8,128)(2,1)S(1)}, u32[]{:S(2)}, u32[]{:S(2)}) collective-permute-start(bf16[2,2,12,8,384]{4,3,2,1,0:T(8,128)(2,1)} %get-tuple-element.14), channel_id=1, source_target_pairs={{0,256},{128,384},{256,0},{384,128},{1,257},{129,385},{257,1},{385... | collective-permute-start | bytes 884744 | tf_op jit(solution)/shard_map/ppermute | solution.py:174
  34.7 21.1 %collective-permute-start.2 = (bf16[2,2,12,8,384]{4,3,2,1,0:T(8,128)(2,1)}, bf16[2,2,12,8,384]{4,3,2,1,0:T(8,128)(2,1)S(1)}, u32[]{:S(2)}, u32[]{:S(2)}) collective-permute-start(bf16[2,2,12,8,384]{4,3,2,1,0:T(8,128)(2,1)} %get-tuple-element.13), channel_id=1, source_target_pairs={{0,384},{128,256},{256,128},{384,0},{1,385},{129,257},{257,129},{3... | collective-permute-start | bytes 884744 | tf_op jit(solution)/shard_map/ppermute | solution.py:174

commit v5 on v4

--- a/solution.py
+++ b/solution.py
@@ -19,7 +19,9 @@
 CX = 4
 XL = 8
 BLOCK = 3 * KZL
+QUARTER = NY // 4
 SENT = CX * SLABS * BLOCK
+PADDED = SENT + 40
 
 
 def dft(rows, cols, length):
@@ -31,8 +33,9 @@
 
 @functools.cache
 def row_table():
-    y = np.arange(YL)[:, None] + np.arange(SLABS)[None, :] * YL
-    return np.concatenate(dft(y.reshape(-1), np.arange(NY), NY), axis=1).astype(jnp.bfloat16)
+    y = (np.arange(YL)[:, None] + np.arange(SLABS // 4)[None, :] * YL).reshape(-1)
+    parts = [np.concatenate(dft(y, np.arange(residue, NY, 4), NY), axis=1) for residue in range(4)]
+    return np.stack(parts).astype(jnp.bfloat16)
 
 
 @functools.cache
@@ -48,7 +51,8 @@
     theta = 2.0 * math.pi / PHASES
     cosine = math.cos(theta)
     sine = math.sin(theta)
-    ky = lax.broadcasted_iota(jnp.int32, (NY, 128), 0)
+    row = lax.broadcasted_iota(jnp.int32, (NY, 128), 0)
+    ky = 4 * (row % QUARTER) + row // QUARTER
     lanes = lax.broadcasted_iota(jnp.int32, (1, 128), 1)
 
     def grid_of(kz):
@@ -71,7 +75,10 @@
         placed = lax.dot_general(
             chosen, samples, (((1,), (1,)), ((), ())), preferred_element_type=jnp.float32
         ).astype(jnp.bfloat16)
-        return jnp.concatenate([placed[:, :128], placed[:, 128:]], axis=0)
+        return [
+            jnp.concatenate([placed[at : at + QUARTER, :128], placed[at : at + QUARTER, 128:]], axis=0)
+            for at in range(0, NY, QUARTER)
+        ]
 
     def exchange(a, b, bit):
         upper = (lanes & bit) != 0
@@ -80,18 +87,36 @@
             jnp.where(upper, b, pltpu.roll(a, 128 - bit, 1)),
         )
 
+    sign = jnp.where(lanes < 64, -1.0, 1.0)
+
+    ahead = grid_of(0), grid_of(1)
     for pair in range(KZL // 2):
-        grids = jnp.concatenate([grid_of(2 * pair), grid_of(2 * pair + 1)], axis=1)
-        both = jnp.dot(w_ref[...], grids, preferred_element_type=jnp.float32)
+        first, second = ahead
+        if pair + 1 < KZL // 2:
+            ahead = grid_of(2 * pair + 2), grid_of(2 * pair + 3)
+        both = [
+            jnp.dot(w_ref[residue], jnp.concatenate([first[residue], second[residue]], axis=1), preferred_element_type=jnp.float32)
+            for residue in range(4)
+        ]
         for half in range(2):
             kz = 2 * pair + half
-            for third in range(3):
-                part = both[third * 128 : third * 128 + 128, half * 128 : half * 128 + 128].astype(jnp.bfloat16)
-                for high, sides in enumerate(exchange(part[:64], part[64:], 16)):
-                    for low, value in enumerate(exchange(sides[:32], sides[32:], 8)):
-                        start = (2 * high + low) * SLABS * BLOCK + third * KZL + kz
-                        scratch[pl.ds(start, SLABS, stride=BLOCK), :] = value.astype(jnp.float32)
-    out_ref[...] = scratch[...].astype(jnp.bfloat16)
+            f0, f1, f2, f3 = (part[:, half * 128 : half * 128 + 128] for part in both)
+            even, odd = f0 + f2, f1 + f3
+            cross, turned = f0 - f2, sign * pltpu.roll(f1 - f3, 64, 1)
+            quarters = (even + odd, cross + turned, even - odd, cross - turned)
+            for side in range(2):
+                for third in range(3):
+                    tiles = []
+                    for y in range(4 * third, 4 * third + 4):
+                        near, far = (q[8 * y : 8 * y + 8] for q in quarters[2 * side : 2 * side + 2])
+                        tiles.append(jnp.concatenate([near, far], axis=0).astype(jnp.bfloat16))
+                    low = exchange(tiles[0], tiles[2], 16)
+                    high = exchange(tiles[1], tiles[3], 16)
+                    for upper in range(2):
+                        for lower, value in enumerate(exchange(low[upper], high[upper], 8)):
+                            start = ((2 * upper + lower) * SLABS + 16 * side) * BLOCK + third * KZL + kz
+                            scratch[pl.ds(start, 16, stride=BLOCK), :] = value.astype(jnp.float32)
+    out_ref[...] = scratch[:SENT].astype(jnp.bfloat16)
 
 
 def encode(kspace, line_index):
@@ -100,13 +125,13 @@
         out_shape=jax.ShapeDtypeStruct((SENT, 128), jnp.bfloat16),
         in_specs=[pl.BlockSpec(memory_space=pltpu.VMEM)] * 3,
         out_specs=pl.BlockSpec(memory_space=pltpu.VMEM),
-        scratch_shapes=[pltpu.VMEM((SENT, 128), jnp.float32)],
+        scratch_shapes=[pltpu.VMEM((PADDED, 128), jnp.float32)],
         name="encode",
     )(jnp.transpose(kspace, (0, 1, 2, 4, 3, 5)), jnp.transpose(line_index, (1, 0, 2)), jnp.asarray(row_table()))
 
 
 def image_kernel(me_ref, r_ref, m0_ref, m1_ref, m2_ref, m3_ref, d_ref, own_ref, other_ref, wide, lhs, sums):
-    wide[...] = r_ref[...].astype(jnp.float32)
+    wide[:SENT] = r_ref[...].astype(jnp.float32)
     column = me_ref[0]
     core = me_ref[1]
     for third in range(3):
@@ -155,9 +180,9 @@
         in_specs=[pl.BlockSpec(memory_space=pltpu.SMEM)] + [vmem] * 6,
         out_specs=(vmem, vmem),
         scratch_shapes=[
-            pltpu.VMEM((SENT, 128), jnp.float32),
+            pltpu.VMEM((PADDED, 128), jnp.float32),
             pltpu.VMEM((3, 4 * 64, 2 * NZ), jnp.bfloat16),
-            pltpu.VMEM((3, 2 * YL * XL, 128), jnp.float32),
+            pltpu.VMEM((3, 2 * YL * (XL + 1), 128), jnp.float32),
         ],
         compiler_params=pltpu.CompilerParams(vmem_limit_bytes=24 << 20),
         name="images",

time: 103 us -> 103 us (level)
  no operation moved by 1% of the time
where the time goes in v5:
time: 103 us
  waiting for transfers between devices  47.1 us (46%)
  starting transfers between devices  30 us (29%)
  blocking collectives  16 us (16%)
  Pallas kernels  6.22 us (6%)
  local copies, waits for them, and re-layouts  3.02 us (3%)
    all_to_all x1, waiting for transfers between devices, local(): lax.all_to_all(sent.reshape(CX * SLABS, BLOCK // 4, 4, 128), ('cx', 'slab...  28.3 us
    all_to_all x1, starting transfers between devices, local(): lax.all_to_all(sent.reshape(CX * SLABS, BLOCK // 4, 4, 128), ('cx', 'slab...  20.4 us
    ppermute x3, waiting for transfers between devices, shared_maps(): chunk = lax.ppermute(chunk, 'cx', [(i, i ^ step) for i in range(CX)])  18.8 us
    all_gather x2, blocking collectives, from_partner(): pair = lax.all_gather(value, axis)  16 us
    ppermute x3, starting transfers between devices, shared_maps(): chunk = lax.ppermute(chunk, 'cx', [(i, i ^ step) for i in range(CX)])  9.57 us
    pallas_call x1, Pallas kernels, encode(): pl.pallas_call(encode_kernel, out_shape=jax.ShapeDtypeStruct((SENT, 128),...  4.14 us
    dynamic_slice x1, local copies, waits for them, and re-layouts, shared_maps(): chunk = lax.dynamic_slice_in_dim(rows, (column ^ step) * XL, XL, axis=3)  2.32 us
    pallas_call x1, Pallas kernels, images(): pl.pallas_call(image_kernel, out_shape=(half, half), in_specs=[pl.BlockSp...  2.08 us
  transfers between devices with their start and end apart: 4, of which 4 were waited for; matrix products, arithmetic and copies ran while one was open for 2% of the time, Pallas kernels for 0%

profile of v5, /device:TPU:1, one launch (start us, length us, event | category | flops | bytes accessed | tf_op | source)
XLA Modules:
  0.0 102.6 jit_solution(8835163220614997967)
XLA Ops:
  0.0 4.1 %encode.1 = bf16[4608,128]{1,0:T(8,128)(2,1)} custom-call(bf16[2,2,2,12,32,128]{5,4,3,2,1,0:T(8,128)(2,1)} %bitcast.21, s32[12,2,128]{2,1,0:T(2,128)} %bitcast.25, bf16[4,96,192]{2,1,0:T(8,128)(2,1)} %constant.48.clone.w_ref), custom_call_target="tpu_custom_call" | custom-call | tf_op jit(solution)/shard_map/encode/pallas_call | solution.py:123
  4.1 20.4 %all-to-all-start = ((bf16[128,9,4,128]{3,2,1,0:T(4,128)(2,1)}), bf16[128,9,4,128]{3,2,1,0:T(4,128)(2,1)S(1)}, u32[]{:S(2)}, u32[]{:S(2)}) async-start(bf16[128,9,4,128]{3,2,1,0:T(4,128)(2,1)} %bitcast.20), calls=%async_computation | async-start | bytes 2359296 | tf_op jit(solution)/shard_map/all_to_all | solution.py:211
  24.6 0.0 copy-start
  24.6 2.3 %dynamic-slice_bitcast_fusion = (bf16[2,2,12,8,384]{4,3,2,1,0:T(8,128)(2,1)}, bf16[2,2,12,8,384]{4,3,2,1,0:T(8,128)(2,1)}, bf16[2,2,12,8,384]{4,3,2,1,0:T(8,128)(2,1)}, bf16[2,2,12,8,384]{4,3,2,1,0:T(8,128)(2,1)S(1)}) fusion(bf16[2,2,32,12,384]{4,2,3,1,0:T(8,128)(2,1)} %param.6, s32[]{:T(128)S(6)} %select_n.28, s32[]{:T(128)S(6)} %select_n.27, ...), kind=kLoop, calls=%fused_computation | loop fusion | bytes 2359312 | tf_op jit(solution)/shard_map/dynamic_slice | solution.py:197
  26.9 2.6 %collective-permute-start = (bf16[2,2,12,8,384]{4,3,2,1,0:T(8,128)(2,1)}, bf16[2,2,12,8,384]{4,3,2,1,0:T(8,128)(2,1)S(1)}, u32[]{:S(2)}, u32[]{:S(2)}) collective-permute-start(bf16[2,2,12,8,384]{4,3,2,1,0:T(8,128)(2,1)} %get-tuple-element.15), channel_id=1, source_target_pairs={{0,128},{128,0},{256,384},{384,256},{1,129},{129,1},{257,385},{385... | collective-permute-start | bytes 884744 | tf_op jit(solution)/shard_map/ppermute | solution.py:199
  29.5 4.7 %collective-permute-start.1 = (bf16[2,2,12,8,384]{4,3,2,1,0:T(8,128)(2,1)}, bf16[2,2,12,8,384]{4,3,2,1,0:T(8,128)(2,1)S(1)}, u32[]{:S(2)}, u32[]{:S(2)}) collective-permute-start(bf16[2,2,12,8,384]{4,3,2,1,0:T(8,128)(2,1)} %get-tuple-element.14), channel_id=1, source_target_pairs={{0,256},{128,384},{256,0},{384,128},{1,257},{129,385},{257,1},{385... | collective-permute-start | bytes 884744 | tf_op jit(solution)/shard_map/ppermute | solution.py:199
  34.2 2.3 %collective-permute-start.2 = (bf16[2,2,12,8,384]{4,3,2,1,0:T(8,128)(2,1)}, bf16[2,2,12,8,384]{4,3,2,1,0:T(8,128)(2,1)S(1)}, u32[]{:S(2)}, u32[]{:S(2)}) collective-permute-start(bf16[2,2,12,8,384]{4,3,2,1,0:T(8,128)(2,1)} %get-tuple-element.13), channel_id=1, source_target_pairs={{0,384},{128,256},{256,128},{384,0},{1,385},{129,257},{257,129},{3... | collective-permute-start | bytes 884744 | tf_op jit(solution)/shard_map/ppermute | solution.py:199
  36.5 0.1 pad_add_fusion.me_ref
  36.6 2.7 %collective-permute-done.m1_ref = bf16[2,2,12,8,384]{4,3,2,1,0:T(8,128)(2,1)S(1)} collective-permute-done((bf16[2,2,12,8,384]{4,3,2,1,0:T(8,128)(2,1)}, bf16[2,2,12,8,384]{4,3,2,1,0:T(8,128)(2,1)S(1)}, u32[]{:S(2)}, u32[]{:S(2)}) %collective-permute-start) | collective-permute-done | bytes 294944 | tf_op jit(solution)/shard_map/ppermute | solution.py:199
  39.3 9.5 %collective-permute-done.1.m2_ref = bf16[2,2,12,8,384]{4,3,2,1,0:T(8,128)(2,1)S(1)} collective-permute-done((bf16[2,2,12,8,384]{4,3,2,1,0:T(8,128)(2,1)}, bf16[2,2,12,8,384]{4,3,2,1,0:T(8,128)(2,1)S(1)}, u32[]{:S(2)}, u32[]{:S(2)}) %collective-permute-start.1) | collective-permute-done | bytes 294944 | tf_op jit(solution)/shard_map/ppermute | solution.py:199
  48.7 6.6 %collective-permute-done.2.m3_ref = bf16[2,2,12,8,384]{4,3,2,1,0:T(8,128)(2,1)S(1)} collective-permute-done((bf16[2,2,12,8,384]{4,3,2,1,0:T(8,128)(2,1)}, bf16[2,2,12,8,384]{4,3,2,1,0:T(8,128)(2,1)S(1)}, u32[]{:S(2)}, u32[]{:S(2)}) %collective-permute-start.2) | collective-permute-done | bytes 294944 | tf_op jit(solution)/shard_map/ppermute | solution.py:199
  55.4 28.3 %all-to-all-done = bf16[128,9,4,128]{3,2,1,0:T(4,128)(2,1)S(1)} async-done(((bf16[128,9,4,128]{3,2,1,0:T(4,128)(2,1)}), bf16[128,9,4,128]{3,2,1,0:T(4,128)(2,1)S(1)}, u32[]{:S(2)}, u32[]{:S(2)}) %all-to-all-start) | async-done | bytes 1179680 | tf_op jit(solution)/shard_map/all_to_all | solution.py:211
  83.7 0.0 copy-done
  83.7 2.1 %images.1 = (f32[96,384]{1,0:T(8,128)S(1)}, f32[96,384]{1,0:T(8,128)S(1)}) custom-call(s32[2]{0:T(128)S(1)} %pad_add_fusion.me_ref, bf16[4608,128]{1,0:T(8,128)(2,1)S(1)} %bitcast.19, bf16[2,2,12,8,384]{4,3,2,1,0:T(8,128)(2,1)S(1)} %get-tuple-element.16.m0_ref, bf16[2,2,12,8,384]{4,3,2,1,0:T(8,128)(2,1)S(1)} %collective-permute-done.m1_ref, ...), custom_call_target="tpu_custom_call" | custom-call | tf_op jit(solution)/shard_map/images/pallas_call | solution.py:177
  85.8 3.4 %all-gather = f32[192,384]{1,0:T(8,128)S(1)} all-gather(f32[96,384]{1,0:T(8,128)S(1)} %get-tuple-element.12), channel_id=2, replica_groups=mesh['cx'=4,'zh'=2,'core'=2,'slab'=32] {'core'}, dimensions={0}, use_global_device_ids=true | all-gather | bytes 442368 | tf_op jit(solution)/shard_map/all_gather | solution.py:205
  89.3 12.6 %all_gather.12 = bf16[2,48,384]{2,1,0:T(8,128)(2,1)S(1)} all-gather(bf16[1,48,384]{2,1,0:T(8,128)(2,1)S(1)} %dynamic-slice_convert_fusion), channel_id=1, replica_groups=mesh['cx'=4,'zh'=2,'core'=2,'slab'=32] {'zh'}, dimensions={0}, use_global_device_ids=true | all-gather | bytes 110592 | tf_op jit(solution)/shard_map/all_gather | solution.py:205
  101.9 0.7 add.46
  (3 shorter events, 0.0 us)
Async XLA Ops:
  4.1 79.6 %all-to-all-start = ((bf16[128,9,4,128]{3,2,1,0:T(4,128)(2,1)}), bf16[128,9,4,128]{3,2,1,0:T(4,128)(2,1)S(1)}, u32[]{:S(2)}, u32[]{:S(2)}) async-start(bf16[128,9,4,128]{3,2,1,0:T(4,128)(2,1)} %bitcast.20), calls=%async_computation | async-start | bytes 2359296 | tf_op jit(solution)/shard_map/all_to_all | solution.py:211
  24.6 59.1 %copy-start = (bf16[768,768]{1,0:T(8,128)(2,1)S(1)}, bf16[768,768]{1,0:T(8,128)(2,1)}, u32[]{:S(2)}) copy-start(bf16[768,768]{1,0:T(8,128)(2,1)} %constant.49.clone.d_ref) | copy-start | bytes 3538948
  26.9 12.4 %collective-permute-start = (bf16[2,2,12,8,384]{4,3,2,1,0:T(8,128)(2,1)}, bf16[2,2,12,8,384]{4,3,2,1,0:T(8,128)(2,1)S(1)}, u32[]{:S(2)}, u32[]{:S(2)}) collective-permute-start(bf16[2,2,12,8,384]{4,3,2,1,0:T(8,128)(2,1)} %get-tuple-element.15), channel_id=1, source_target_pairs={{0,128},{128,0},{256,384},{384,256},{1,129},{129,1},{257,385},{385... | collective-permute-start | bytes 884744 | tf_op jit(solution)/shard_map/ppermute | solution.py:199
  29.5 19.2 %collective-permute-start.1 = (bf16[2,2,12,8,384]{4,3,2,1,0:T(8,128)(2,1)}, bf16[2,2,12,8,384]{4,3,2,1,0:T(8,128)(2,1)S(1)}, u32[]{:S(2)}, u32[]{:S(2)}) collective-permute-start(bf16[2,2,12,8,384]{4,3,2,1,0:T(8,128)(2,1)} %get-tuple-element.14), channel_id=1, source_target_pairs={{0,256},{128,384},{256,0},{384,128},{1,257},{129,385},{257,1},{385... | collective-permute-start | bytes 884744 | tf_op jit(solution)/shard_map/ppermute | solution.py:199
  34.2 21.1 %collective-permute-start.2 = (bf16[2,2,12,8,384]{4,3,2,1,0:T(8,128)(2,1)}, bf16[2,2,12,8,384]{4,3,2,1,0:T(8,128)(2,1)S(1)}, u32[]{:S(2)}, u32[]{:S(2)}) collective-permute-start(bf16[2,2,12,8,384]{4,3,2,1,0:T(8,128)(2,1)} %get-tuple-element.13), channel_id=1, source_target_pairs={{0,384},{128,256},{256,128},{384,0},{1,385},{129,257},{257,129},{3... | collective-permute-start | bytes 884744 | tf_op jit(solution)/shard_map/ppermute | solution.py:199

commit v6 on v5

--- a/solution.py
+++ b/solution.py
@@ -21,7 +21,9 @@
 BLOCK = 3 * KZL
 QUARTER = NY // 4
 SENT = CX * SLABS * BLOCK
-PADDED = SENT + 40
+APART = CX * BLOCK
+SPREAD = APART + 4
+PADDED = (SLABS + 2) * SPREAD
 
 
 def dft(rows, cols, length):
@@ -114,9 +116,10 @@
                     high = exchange(tiles[1], tiles[3], 16)
                     for upper in range(2):
                         for lower, value in enumerate(exchange(low[upper], high[upper], 8)):
-                            start = ((2 * upper + lower) * SLABS + 16 * side) * BLOCK + third * KZL + kz
-                            scratch[pl.ds(start, 16, stride=BLOCK), :] = value.astype(jnp.float32)
-    out_ref[...] = scratch[:SENT].astype(jnp.bfloat16)
+                            start = (2 * upper + lower) * BLOCK + 16 * side * SPREAD + third * KZL + kz
+                            scratch[pl.ds(start, 16, stride=SPREAD), :] = value.astype(jnp.float32)
+    for slab in range(SLABS):
+        out_ref[slab * APART : (slab + 1) * APART] = scratch[slab * SPREAD : slab * SPREAD + APART].astype(jnp.bfloat16)
 
 
 def encode(kspace, line_index):
@@ -131,14 +134,15 @@
 
 
 def image_kernel(me_ref, r_ref, m0_ref, m1_ref, m2_ref, m3_ref, d_ref, own_ref, other_ref, wide, lhs, sums):
-    wide[:SENT] = r_ref[...].astype(jnp.float32)
+    for slab in range(SLABS):
+        wide[slab * SPREAD : slab * SPREAD + APART] = r_ref[slab * APART : (slab + 1) * APART].astype(jnp.float32)
     column = me_ref[0]
     core = me_ref[1]
     for third in range(3):
         for step in range(CX):
-            base = (column ^ step) * (SLABS * BLOCK)
+            base = (column ^ step) * BLOCK
             rows = jnp.concatenate(
-                [wide[pl.ds(base + third * KZL + kz, SLABS, stride=BLOCK), :] for kz in range(KZL)], axis=0
+                [wide[pl.ds(base + third * KZL + kz, SLABS, stride=SPREAD), :] for kz in range(KZL)], axis=0
             )
             turned = rows.T.astype(jnp.bfloat16)
             lhs[third, step * 64 : step * 64 + 64, : KZL * SLABS] = turned[:64]
@@ -209,7 +213,7 @@
 def local(kspace, coil_maps, line_index):
     sent, coil_maps = lax.optimization_barrier((encode(kspace, line_index), coil_maps))
     arrived = lax.all_to_all(
-        sent.reshape(CX * SLABS, BLOCK // 4, 4, 128), ("cx", "slab"), split_axis=0, concat_axis=0, tiled=True
+        sent.reshape(CX * SLABS, BLOCK // 4, 4, 128), ("slab", "cx"), split_axis=0, concat_axis=0, tiled=True
     ).reshape(SENT, 128)
     own, other = images(arrived, shared_maps(coil_maps))
     pairs = (own + from_partner(other, "core")).reshape(2, 4 * YL, NZ)

time: 103 us -> 101 us (0.981)
  waiting for transfers between devices: 47.1 us -> 45.2 us
    all_to_all x1, waiting for transfers between devices: 28.3 us -> 26.2 us  [local(): lax.all_to_all(sent.reshape(CX * SLABS, BLOCK // 4, 4, 128), ('slab', 'cx...]
where the time goes in v6:
time: 101 us
  waiting for transfers between devices  45.2 us (45%)
  starting transfers between devices  30 us (30%)
  blocking collectives  16.1 us (16%)
  Pallas kernels  6.22 us (6%)
  local copies, waits for them, and re-layouts  3.02 us (3%)
    all_to_all x1, waiting for transfers between devices, local(): lax.all_to_all(sent.reshape(CX * SLABS, BLOCK // 4, 4, 128), ('slab', 'cx...  26.2 us
    all_to_all x1, starting transfers between devices, local(): lax.all_to_all(sent.reshape(CX * SLABS, BLOCK // 4, 4, 128), ('slab', 'cx...  20.4 us
    ppermute x3, waiting for transfers between devices, shared_maps(): chunk = lax.ppermute(chunk, 'cx', [(i, i ^ step) for i in range(CX)])  19 us
    all_gather x2, blocking collectives, from_partner(): pair = lax.all_gather(value, axis)  16.1 us
    ppermute x3, starting transfers between devices, shared_maps(): chunk = lax.ppermute(chunk, 'cx', [(i, i ^ step) for i in range(CX)])  9.57 us
    pallas_call x1, Pallas kernels, encode(): pl.pallas_call(encode_kernel, out_shape=jax.ShapeDtypeStruct((SENT, 128),...  4.14 us
    dynamic_slice x1, local copies, waits for them, and re-layouts, shared_maps(): chunk = lax.dynamic_slice_in_dim(rows, (column ^ step) * XL, XL, axis=3)  2.32 us
    pallas_call x1, Pallas kernels, images(): pl.pallas_call(image_kernel, out_shape=(half, half), in_specs=[pl.BlockSp...  2.08 us
  transfers between devices with their start and end apart: 4, of which 4 were waited for; matrix products, arithmetic and copies ran while one was open for 2% of the time, Pallas kernels for 0%

profile of v6, /device:TPU:1, one launch (start us, length us, event | category | flops | bytes accessed | tf_op | source)
XLA Modules:
  0.0 100.6 jit_solution(8162570717075863453)
XLA Ops:
  0.0 4.1 %encode.1 = bf16[4608,128]{1,0:T(8,128)(2,1)} custom-call(bf16[2,2,2,12,32,128]{5,4,3,2,1,0:T(8,128)(2,1)} %bitcast.21, s32[12,2,128]{2,1,0:T(2,128)} %bitcast.25, bf16[4,96,192]{2,1,0:T(8,128)(2,1)} %constant.48.clone.w_ref), custom_call_target="tpu_custom_call" | custom-call | tf_op jit(solution)/shard_map/encode/pallas_call | solution.py:126
  4.1 20.4 %all-to-all-start = ((bf16[128,9,4,128]{3,2,1,0:T(4,128)(2,1)}), bf16[128,9,4,128]{3,2,1,0:T(4,128)(2,1)S(1)}, u32[]{:S(2)}, u32[]{:S(2)}) async-start(bf16[128,9,4,128]{3,2,1,0:T(4,128)(2,1)} %bitcast.20), calls=%async_computation | async-start | bytes 2359296 | tf_op jit(solution)/shard_map/all_to_all | solution.py:215
  24.6 0.0 copy-start
  24.6 2.3 %dynamic-slice_bitcast_fusion = (bf16[2,2,12,8,384]{4,3,2,1,0:T(8,128)(2,1)}, bf16[2,2,12,8,384]{4,3,2,1,0:T(8,128)(2,1)}, bf16[2,2,12,8,384]{4,3,2,1,0:T(8,128)(2,1)}, bf16[2,2,12,8,384]{4,3,2,1,0:T(8,128)(2,1)S(1)}) fusion(bf16[2,2,32,12,384]{4,2,3,1,0:T(8,128)(2,1)} %param.6, s32[]{:T(128)S(6)} %select_n.28, s32[]{:T(128)S(6)} %select_n.27, ...), kind=kLoop, calls=%fused_computation | loop fusion | bytes 2359312 | tf_op jit(solution)/shard_map/dynamic_slice | solution.py:201
  26.9 2.5 %collective-permute-start = (bf16[2,2,12,8,384]{4,3,2,1,0:T(8,128)(2,1)}, bf16[2,2,12,8,384]{4,3,2,1,0:T(8,128)(2,1)S(1)}, u32[]{:S(2)}, u32[]{:S(2)}) collective-permute-start(bf16[2,2,12,8,384]{4,3,2,1,0:T(8,128)(2,1)} %get-tuple-element.15), channel_id=1, source_target_pairs={{0,128},{128,0},{256,384},{384,256},{1,129},{129,1},{257,385},{385... | collective-permute-start | bytes 884744 | tf_op jit(solution)/shard_map/ppermute | solution.py:203
  29.4 4.3 %collective-permute-start.1 = (bf16[2,2,12,8,384]{4,3,2,1,0:T(8,128)(2,1)}, bf16[2,2,12,8,384]{4,3,2,1,0:T(8,128)(2,1)S(1)}, u32[]{:S(2)}, u32[]{:S(2)}) collective-permute-start(bf16[2,2,12,8,384]{4,3,2,1,0:T(8,128)(2,1)} %get-tuple-element.14), channel_id=1, source_target_pairs={{0,256},{128,384},{256,0},{384,128},{1,257},{129,385},{257,1},{385... | collective-permute-start | bytes 884744 | tf_op jit(solution)/shard_map/ppermute | solution.py:203
  33.7 2.8 %collective-permute-start.2 = (bf16[2,2,12,8,384]{4,3,2,1,0:T(8,128)(2,1)}, bf16[2,2,12,8,384]{4,3,2,1,0:T(8,128)(2,1)S(1)}, u32[]{:S(2)}, u32[]{:S(2)}) collective-permute-start(bf16[2,2,12,8,384]{4,3,2,1,0:T(8,128)(2,1)} %get-tuple-element.13), channel_id=1, source_target_pairs={{0,384},{128,256},{256,128},{384,0},{1,385},{129,257},{257,129},{3... | collective-permute-start | bytes 884744 | tf_op jit(solution)/shard_map/ppermute | solution.py:203
  36.5 0.1 pad_add_fusion.me_ref
  36.6 2.2 %collective-permute-done.m1_ref = bf16[2,2,12,8,384]{4,3,2,1,0:T(8,128)(2,1)S(1)} collective-permute-done((bf16[2,2,12,8,384]{4,3,2,1,0:T(8,128)(2,1)}, bf16[2,2,12,8,384]{4,3,2,1,0:T(8,128)(2,1)S(1)}, u32[]{:S(2)}, u32[]{:S(2)}) %collective-permute-start) | collective-permute-done | bytes 294944 | tf_op jit(solution)/shard_map/ppermute | solution.py:203
  38.8 10.0 %collective-permute-done.1.m2_ref = bf16[2,2,12,8,384]{4,3,2,1,0:T(8,128)(2,1)S(1)} collective-permute-done((bf16[2,2,12,8,384]{4,3,2,1,0:T(8,128)(2,1)}, bf16[2,2,12,8,384]{4,3,2,1,0:T(8,128)(2,1)S(1)}, u32[]{:S(2)}, u32[]{:S(2)}) %collective-permute-start.1) | collective-permute-done | bytes 294944 | tf_op jit(solution)/shard_map/ppermute | solution.py:203
  48.8 6.8 %collective-permute-done.2.m3_ref = bf16[2,2,12,8,384]{4,3,2,1,0:T(8,128)(2,1)S(1)} collective-permute-done((bf16[2,2,12,8,384]{4,3,2,1,0:T(8,128)(2,1)}, bf16[2,2,12,8,384]{4,3,2,1,0:T(8,128)(2,1)S(1)}, u32[]{:S(2)}, u32[]{:S(2)}) %collective-permute-start.2) | collective-permute-done | bytes 294944 | tf_op jit(solution)/shard_map/ppermute | solution.py:203
  55.6 26.2 %all-to-all-done = bf16[128,9,4,128]{3,2,1,0:T(4,128)(2,1)S(1)} async-done(((bf16[128,9,4,128]{3,2,1,0:T(4,128)(2,1)}), bf16[128,9,4,128]{3,2,1,0:T(4,128)(2,1)S(1)}, u32[]{:S(2)}, u32[]{:S(2)}) %all-to-all-start) | async-done | bytes 1179680 | tf_op jit(solution)/shard_map/all_to_all | solution.py:215
  81.8 0.0 copy-done
  81.8 2.1 %images.1 = (f32[96,384]{1,0:T(8,128)S(1)}, f32[96,384]{1,0:T(8,128)S(1)}) custom-call(s32[2]{0:T(128)S(1)} %pad_add_fusion.me_ref, bf16[4608,128]{1,0:T(8,128)(2,1)S(1)} %bitcast.19, bf16[2,2,12,8,384]{4,3,2,1,0:T(8,128)(2,1)S(1)} %get-tuple-element.16.m0_ref, bf16[2,2,12,8,384]{4,3,2,1,0:T(8,128)(2,1)S(1)} %collective-permute-done.m1_ref, ...), custom_call_target="tpu_custom_call" | custom-call | tf_op jit(solution)/shard_map/images/pallas_call | solution.py:181
  83.8 3.8 %all-gather = f32[192,384]{1,0:T(8,128)S(1)} all-gather(f32[96,384]{1,0:T(8,128)S(1)} %get-tuple-element.12), channel_id=2, replica_groups=mesh['cx'=4,'zh'=2,'core'=2,'slab'=32] {'core'}, dimensions={0}, use_global_device_ids=true | all-gather | bytes 442368 | tf_op jit(solution)/shard_map/all_gather | solution.py:209
  87.7 12.3 %all_gather.12 = bf16[2,48,384]{2,1,0:T(8,128)(2,1)S(1)} all-gather(bf16[1,48,384]{2,1,0:T(8,128)(2,1)S(1)} %dynamic-slice_convert_fusion), channel_id=1, replica_groups=mesh['cx'=4,'zh'=2,'core'=2,'slab'=32] {'zh'}, dimensions={0}, use_global_device_ids=true | all-gather | bytes 110592 | tf_op jit(solution)/shard_map/all_gather | solution.py:209
  100.0 0.7 add.46
  (3 shorter events, 0.0 us)
Async XLA Ops:
  4.1 77.6 %all-to-all-start = ((bf16[128,9,4,128]{3,2,1,0:T(4,128)(2,1)}), bf16[128,9,4,128]{3,2,1,0:T(4,128)(2,1)S(1)}, u32[]{:S(2)}, u32[]{:S(2)}) async-start(bf16[128,9,4,128]{3,2,1,0:T(4,128)(2,1)} %bitcast.20), calls=%async_computation | async-start | bytes 2359296 | tf_op jit(solution)/shard_map/all_to_all | solution.py:215
  24.6 57.2 %copy-start = (bf16[768,768]{1,0:T(8,128)(2,1)S(1)}, bf16[768,768]{1,0:T(8,128)(2,1)}, u32[]{:S(2)}) copy-start(bf16[768,768]{1,0:T(8,128)(2,1)} %constant.49.clone.d_ref) | copy-start | bytes 3538948
  26.9 11.9 %collective-permute-start = (bf16[2,2,12,8,384]{4,3,2,1,0:T(8,128)(2,1)}, bf16[2,2,12,8,384]{4,3,2,1,0:T(8,128)(2,1)S(1)}, u32[]{:S(2)}, u32[]{:S(2)}) collective-permute-start(bf16[2,2,12,8,384]{4,3,2,1,0:T(8,128)(2,1)} %get-tuple-element.15), channel_id=1, source_target_pairs={{0,128},{128,0},{256,384},{384,256},{1,129},{129,1},{257,385},{385... | collective-permute-start | bytes 884744 | tf_op jit(solution)/shard_map/ppermute | solution.py:203
  29.4 19.4 %collective-permute-start.1 = (bf16[2,2,12,8,384]{4,3,2,1,0:T(8,128)(2,1)}, bf16[2,2,12,8,384]{4,3,2,1,0:T(8,128)(2,1)S(1)}, u32[]{:S(2)}, u32[]{:S(2)}) collective-permute-start(bf16[2,2,12,8,384]{4,3,2,1,0:T(8,128)(2,1)} %get-tuple-element.14), channel_id=1, source_target_pairs={{0,256},{128,384},{256,0},{384,128},{1,257},{129,385},{257,1},{385... | collective-permute-start | bytes 884744 | tf_op jit(solution)/shard_map/ppermute | solution.py:203
  33.7 21.9 %collective-permute-start.2 = (bf16[2,2,12,8,384]{4,3,2,1,0:T(8,128)(2,1)}, bf16[2,2,12,8,384]{4,3,2,1,0:T(8,128)(2,1)S(1)}, u32[]{:S(2)}, u32[]{:S(2)}) collective-permute-start(bf16[2,2,12,8,384]{4,3,2,1,0:T(8,128)(2,1)} %get-tuple-element.13), channel_id=1, source_target_pairs={{0,384},{128,256},{256,128},{384,0},{1,385},{129,257},{257,129},{3... | collective-permute-start | bytes 884744 | tf_op jit(solution)/shard_map/ppermute | solution.py:203
